TPU v7x, 512 devices: a whole 4x4x16 slice. The times are simulated.
512 devices in a mesh: track: 64 (over y_hi, z, core), chan: 8 (over x, y_lo).
Axes of the slice: x: 4, y: 4 (y_hi: 2, y_lo: 2; y = y_hi * 2 + y_lo), z: 16, core: 2. Of those that a mesh axis runs over, the one named last changes fastest.
Arguments:
- radiance: bfloat16 [256, 30, 72, 128], P('track', None, 'chan'), may hold values from -600 to 600
- w_key: bfloat16 [72, 128, 128], P('chan'), may hold values from -0.5 to 0.5
- w_value: bfloat16 [72, 128, 128], P('chan'), may hold values from -0.5 to 0.5
- latent_query: bfloat16 [64, 512], replicated, may hold values from -6 to 6
- band_blocks: int32 [8, 48], replicated, may hold values from 0 to 71, as said below
- band_count: int32 [8], replicated, may hold values from 24 to 48
- valid_mask: int32 [256, 30, 9], P('track'), may hold values 0 or 1
- w_out: bfloat16 [512, 512], replicated, may hold values from -0.25 to 0.25
- conv_taps: float32 [3, 9, 512], replicated, may hold values from -2.5 to 2.5
- w_mix: bfloat16 [3, 512, 512], replicated, may hold values from -0.25 to 0.25
Outputs:
- cleared: bfloat16 [256, 30, 64, 512], P('track', None, 'chan')
Inputs may be any that keep to these rules, and one draw needn't show every extreme that they name: `band_blocks`: within a row all entries are distinct; group g uses the first band_count[g] of them.
All inputs are finite; a program needn't handle non-finite values. No bound on the sum of `valid_mask` on one device may be relied on, other than what follows from the above.
Results may differ from a plain program's by a relative error of at most 0.0095.
Values may be sent and summed in bfloat16 or wider, within the bound.
A program may use at most 64 MiB of HBM per device.

v0:
```python
import jax
import jax.numpy as jnp
from jax import lax
from jax.sharding import PartitionSpec as P

HEADS = 8
HEAD_DIM = 64
KV_HEADS = 2
LAT_GROUP = 8
NBLK = 72
CC_LAYERS = 3


def with_halo(value, sides, width):
    for axis, dim in sides:
        count, length = (lax.axis_size(axis), value.shape[dim])
        up = [(i, (i + 1) % count) for i in range(count - 1)]
        down = [(j, i) for i, j in up]
        last = lax.slice_in_dim(value, length - width, length, axis=dim)
        leading = lax.slice_in_dim(value, 0, width, axis=dim)
        before = lax.ppermute(last, axis, up)
        after = lax.ppermute(leading, axis, down)
        value = jnp.concatenate([before, value, after], axis=dim)
    return value


def band_table(band_blocks, band_count):
    slot_index = jnp.arange(band_blocks.shape[1], dtype=jnp.int32)
    in_use = slot_index[None, :] < band_count[:, None]
    block_index = jnp.arange(NBLK, dtype=jnp.int32)
    matches = (band_blocks[:, :, None] == block_index[None, None, :]) & in_use[:, :, None]
    return jnp.any(matches, axis=1)


def project_blocks(radiance_rows, w_key, w_value):
    key_rows = jnp.einsum(
        "fnc,nck->fnk", radiance_rows, w_key, preferred_element_type=jnp.float32
    ).astype(jnp.bfloat16)
    values32 = radiance_rows.astype(jnp.float32)
    inverse = lax.rsqrt(jnp.mean(values32 * values32, axis=-1, keepdims=True) + 1e-05)
    normed = (values32 * inverse).astype(jnp.bfloat16)
    value_rows = jnp.einsum(
        "fnc,nck->fnk", normed, w_value, preferred_element_type=jnp.float32
    ).astype(jnp.bfloat16)
    return (key_rows, value_rows)


def empty_state(footprints, latent_count):
    repeat = HEADS // KV_HEADS
    running_peak = jnp.full((footprints, latent_count, KV_HEADS, repeat, 1), -1e30, jnp.float32)
    weight_sum = jnp.zeros((footprints, latent_count, KV_HEADS, repeat, 1), jnp.float32)
    weighted = jnp.zeros((footprints, latent_count, KV_HEADS, repeat, HEAD_DIM), jnp.float32)
    return (running_peak, weight_sum, weighted)


def online_update(state_now, queries, key_rows, value_rows, allowed_piece):
    running_peak, weight_sum, weighted = state_now
    repeat = HEADS // KV_HEADS
    footprints, block_count = (key_rows.shape[0], key_rows.shape[1])
    query_heads = queries.reshape(queries.shape[0], KV_HEADS, repeat, HEAD_DIM)
    key_heads = key_rows.reshape(footprints, block_count, KV_HEADS, HEAD_DIM)
    value_heads = value_rows.astype(jnp.float32).reshape(
        footprints, block_count, KV_HEADS, HEAD_DIM
    )
    scores = jnp.einsum(
        "lgrd,fngd->flgrn", query_heads, key_heads, preferred_element_type=jnp.float32
    ) * HEAD_DIM ** (-0.5)
    allowed_now = allowed_piece[None, :, None, None, :]
    scores = jnp.where(allowed_now, scores, -1e30)
    new_peak = jnp.maximum(running_peak, jnp.max(scores, axis=-1, keepdims=True))
    weights = jnp.where(allowed_now, jnp.exp(scores - new_peak), 0.0)
    weight_sum = jnp.sum(weights, axis=-1, keepdims=True)
    weighted = jnp.einsum(
        "flgrn,fngd->flgrd", weights, value_heads, precision=lax.Precision.HIGHEST
    )
    return (new_peak, weight_sum, weighted)


def finish_state(state_now):
    running_peak, weight_sum, weighted = state_now
    footprints, latent_count = (weighted.shape[0], weighted.shape[1])
    return (
        (weighted / weight_sum)
        .reshape(footprints, latent_count, HEADS * HEAD_DIM)
        .astype(jnp.bfloat16)
    )


def add_output(queries, attended, w_out):
    mixed_term = jnp.dot(
        attended.reshape(-1, attended.shape[-1]), w_out, preferred_element_type=jnp.float32
    )
    mixed_term = mixed_term.reshape(attended.shape)
    return (queries.astype(jnp.float32)[None] + mixed_term).astype(jnp.bfloat16)


def clear_layer(latent_grid, valid_mask, taps, w_mix):
    line_count, scan_width = (latent_grid.shape[0], latent_grid.shape[1])
    rimmed = with_halo(latent_grid, (("track", 0),), 1)
    padded = jnp.pad(rimmed, ((0, 0), (1, 1), (0, 0), (0, 0)))
    validity = valid_mask.astype(jnp.float32)
    gathered = jnp.zeros(latent_grid.shape, jnp.float32)
    for offset in range(9):
        row_step, col_step = (offset // 3, offset % 3)
        beside = padded[row_step : row_step + line_count, col_step : col_step + scan_width].astype(
            jnp.float32
        )
        gathered = gathered + validity[:, :, offset][:, :, None, None] * taps[offset] * beside
    mixed_term = gathered.astype(jnp.bfloat16)
    update = jnp.dot(
        mixed_term.reshape(-1, mixed_term.shape[-1]), w_mix, preferred_element_type=jnp.float32
    )
    update = update.reshape(gathered.shape)
    return (latent_grid.astype(jnp.float32) + update).astype(jnp.bfloat16)


def local(
    radiance,
    w_key,
    w_value,
    latent_query,
    band_blocks,
    band_count,
    valid_mask,
    w_out,
    conv_taps,
    w_mix,
):
    line_count, scan_width, blocks_here, channels = radiance.shape
    chan_count = lax.axis_size("chan")
    chan_index = lax.axis_index("chan")
    latent_total, model_width = latent_query.shape
    latents_here = latent_total // chan_count
    footprints = line_count * scan_width
    allowed_lat = jnp.repeat(band_table(band_blocks, band_count), LAT_GROUP, axis=0)
    radiance_rows = radiance.reshape(footprints, blocks_here, channels)
    queries_here = lax.dynamic_slice_in_dim(
        latent_query, chan_index * latents_here, latents_here, 0
    )
    allowed_here = lax.dynamic_slice_in_dim(allowed_lat, chan_index * latents_here, latents_here, 0)
    key_rows, value_rows = project_blocks(radiance_rows, w_key, w_value)
    piece_keys = lax.all_gather(key_rows, "chan", axis=1, tiled=True)
    piece_values = lax.all_gather(value_rows, "chan", axis=1, tiled=True)
    state_now = online_update(
        empty_state(footprints, latents_here), queries_here, piece_keys, piece_values, allowed_here
    )
    latents = add_output(queries_here, finish_state(state_now), w_out)
    latent_grid = latents.reshape(line_count, scan_width, latents_here, model_width)
    for layer_index in range(CC_LAYERS):
        latent_grid = clear_layer(
            latent_grid, valid_mask, conv_taps[layer_index], w_mix[layer_index]
        )
    return latent_grid


def solution(mesh):
    return jax.shard_map(
        local,
        mesh=mesh,
        in_specs=(
            P("track", None, "chan", None),
            P("chan", None, None),
            P("chan", None, None),
            P(),
            P(),
            P(),
            P("track", None, None),
            P(),
            P(),
            P(),
        ),
        out_specs=P("track", None, "chan", None),
        check_vma=False,
    )
```

profile of v0, /device:TPU:24, one launch (start us, length us, event | category | flops | bytes accessed | tf_op | source)
XLA Modules:
  0.0 212.2 jit_solution(15049985069283046947)
XLA Ops:
  6.5 1.1 copy.59
  7.8 2.0 fusion.27
  10.5 1.1 fusion.26
  11.6 0.7 fusion.93
  14.7 1.3 broadcast_multiply_fusion.2
  16.0 1.3 broadcast_multiply_fusion.6
  17.4 1.4 broadcast_multiply_fusion.4
  18.8 56.0 %all-gather.5.cloned.1.call-done = bf16[120,72,128]{2,0,1:T(8,128)(2,1)} async-done(((bf16[120,9,128]{2,0,1:T(8,128)(2,1)}), bf16[120,72,128]{2,0,1:T(8,128)(2,1)}) %all-gather.5.cloned.1.call-update) | async-done | bytes 2211856 | tf_op jit(solution)/shard_map/all_gather | solution.py:142
  74.8 3.0 %copy.63 = bf16[120,72,128]{0,2,1:T(8,128)(2,1)S(1)} copy(bf16[120,72,128]{2,0,1:T(8,128)(2,1)} %all-gather.5.cloned.1.call-done) | data formatting | bytes 4423680 | tf_op jit(solution)/shard_map/all_gather | solution.py:142
  78.3 0.7 fusion.94
  79.0 4.5 %copy.67 = f32[120,8,2,4,72]{4,1,3,2,0:T(8,128)} copy(f32[120,8,2,4,72]{0,1,3,4,2:T(8,128)S(1)} %get-tuple-element.8) | data formatting | bytes 4423680 | tf_op jit(solution)/shard_map/jit(_where)/select_n | solution.py:71
  83.7 54.7 %all-gather.3.cloned.1.call-done = bf16[120,72,128]{2,0,1:T(8,128)(2,1)} async-done(((bf16[120,9,128]{2,0,1:T(8,128)(2,1)}), bf16[120,72,128]{2,0,1:T(8,128)(2,1)}) %all-gather.3.cloned.1.call-update) | async-done | bytes 2211856 | tf_op jit(solution)/shard_map/all_gather | solution.py:143
  138.5 5.6 %copy.77 = bf16[120,72,128]{1,2,0:T(8,128)(2,1)} copy(bf16[120,72,128]{2,0,1:T(8,128)(2,1)} %all-gather.3.cloned.1.call-done) | data formatting | bytes 4423680 | tf_op jit(solution)/shard_map/reshape | solution.py:62
  144.1 9.5 %fusion = bf16[120,8,2,4,64]{4,1,3,2,0:T(8,128)(2,1)S(1)} fusion(bf16[120,72,2,64,1]{1,3,4,2,0:T(8,128)(2,1)} %bitcast.113, f32[120,8,2,4,72]{4,1,3,2,0:T(8,128)} %copy.67, f32[120,8,2,4]{1,3,2,0:T(4,128)S(1)} %copy.68), kind=kOutput, calls=%fused_computation.3 | convolution fusion | flops 425656320 | bytes 5437440 | tf_op jit(solution)/shard_map/flgrn,fngd->flgrd/dot_general | solution.py:73
  153.6 2.0 copy.69
  155.6 0.9 copy.70
  156.6 0.7 add_convert_fusion
  157.3 1.9 collective-permute-start
  159.3 7.3 %collective-permute-start.1 = (bf16[1,30,8,512]{3,2,1,0:T(8,128)(2,1)S(1)}, bf16[1,30,8,512]{3,2,1,0:T(8,128)(2,1)S(1)}, u32[]{:S(2)}, u32[]{:S(2)}) collective-permute-start(bf16[1,30,8,512]{3,2,1,0:T(8,128)(2,1)S(1)} %get-tuple-element.14), channel_id=1, source_target_pairs={{8,0},{16,8},{24,16},{32,24},{40,32},{48,40},{56,48},{64,56},{72,6... | collective-permute-start | bytes 737288 | tf_op jit(solution)/shard_map/ppermute | solution.py:22
  167.0 1.4 collective-permute-done
  168.5 1.8 collective-permute-done.1
  170.5 2.5 %fusion.11 = bf16[4,30,8,512]{3,2,1,0:T(8,128)(2,1)S(1)} fusion(bf16[4,30,8,512]{3,2,1,0:T(8,128)(2,1)S(1)} %bitcast.116, bf16[6,32,8,512]{3,2,1,0:T(8,128)(2,1)S(1)} %select_maximum_fusion.4, bf16[1,30,8,512]{3,2,1,0:T(8,128)(2,1)S(1)} %collective-permute-done.1, bf16[1,30,8,512]{3,2,1,0:T(8,128)(2,1)S(1)} %collective-permute-done, ...), kind=kOutput, calls=%fused_computation.22 | convolution fusion | flops 519045120 | bytes 12222464 | tf_op jit(solution)/shard_map/dot_general | solution.py:110
  173.1 2.1 collective-permute-start.2
  175.2 7.4 %collective-permute-start.3 = (bf16[1,30,8,512]{3,2,1,0:T(8,128)(2,1)S(1)}, bf16[1,30,8,512]{3,2,1,0:T(8,128)(2,1)S(1)}, u32[]{:S(2)}, u32[]{:S(2)}) collective-permute-start(bf16[1,30,8,512]{3,2,1,0:T(8,128)(2,1)S(1)} %get-tuple-element.12), channel_id=1, source_target_pairs={{8,0},{16,8},{24,16},{32,24},{40,32},{48,40},{56,48},{64,56},{72,6... | collective-permute-start | bytes 737288 | tf_op jit(solution)/shard_map/ppermute | solution.py:22
  182.6 1.9 collective-permute-done.2
  184.5 1.8 collective-permute-done.3
  186.5 2.4 %fusion.18 = bf16[4,30,8,512]{3,2,1,0:T(8,128)(2,1)S(1)} fusion(bf16[4,30,8,512]{3,2,1,0:T(8,128)(2,1)S(1)} %fusion.11, bf16[6,32,8,512]{3,2,1,0:T(8,128)(2,1)S(1)} %select_maximum_fusion.2, bf16[1,30,8,512]{3,2,1,0:T(8,128)(2,1)S(1)} %collective-permute-done.3, bf16[1,30,8,512]{3,2,1,0:T(8,128)(2,1)S(1)} %collective-permute-done.2, ...), kind=kOutput, calls=%fused_computation.29 | convolution fusion | flops 519045120 | bytes 12222464 | tf_op jit(solution)/shard_map/dot_general | solution.py:110
  189.0 2.1 collective-permute-start.4
  191.0 7.4 %collective-permute-start.5 = (bf16[1,30,8,512]{3,2,1,0:T(8,128)(2,1)S(1)}, bf16[1,30,8,512]{3,2,1,0:T(8,128)(2,1)S(1)}, u32[]{:S(2)}, u32[]{:S(2)}) collective-permute-start(bf16[1,30,8,512]{3,2,1,0:T(8,128)(2,1)S(1)} %get-tuple-element.10), channel_id=1, source_target_pairs={{8,0},{16,8},{24,16},{32,24},{40,32},{48,40},{56,48},{64,56},{72,6... | collective-permute-start | bytes 737288 | tf_op jit(solution)/shard_map/ppermute | solution.py:22
  198.5 1.9 collective-permute-done.4
  200.4 1.8 collective-permute-done.5
  202.4 3.0 %fusion.25 = bf16[4,30,8,512]{3,2,1,0:T(8,128)(2,1)} fusion(bf16[4,30,8,512]{3,2,1,0:T(8,128)(2,1)S(1)} %fusion.18, bf16[6,32,8,512]{3,2,1,0:T(8,128)(2,1)S(1)} %select_maximum_fusion, bf16[1,30,8,512]{3,2,1,0:T(8,128)(2,1)S(1)} %collective-permute-done.5, bf16[1,30,8,512]{3,2,1,0:T(8,128)(2,1)S(1)} %collective-permute-done.4, ...), kind=kOutput, calls=%fused_computation.36 | convolution fusion | flops 519045120 | bytes 12222464 | tf_op jit(solution)/shard_map/dot_general | solution.py:110
  (106 shorter events, 4.9 us)
Async XLA Ops:
  6.5 150.0 %copy-start = (bf16[512,512]{1,0:T(8,128)(2,1)S(1)}, bf16[512,512]{1,0:T(8,128)(2,1)}, u32[]{:S(2)}) copy-start(bf16[512,512]{1,0:T(8,128)(2,1)} %param.17) | copy-start | bytes 1572868
  6.5 68.2 %all-gather.5.cloned.1.call-start = ((), (), s32[]{:S(2)}) async-start(), calls=%async_computation.1 | async-start | bytes 2488320 | tf_op jit(solution)/shard_map/all_gather | solution.py:142
  9.8 128.7 %all-gather.3.cloned.1.call-start = ((), (), s32[]{:S(2)}) async-start(), calls=%async_computation | async-start | bytes 2488320 | tf_op jit(solution)/shard_map/all_gather | solution.py:143
  156.5 10.0 %copy-start.25 = (f32[4,30]{1,0:T(4,128)S(1)}, f32[4,30]{1,0:T(4,128)}, u32[]{:S(2)}) copy-start(f32[4,30]{1,0:T(4,128)} %get-tuple-element.43) | copy-start | bytes 1444
  156.5 10.0 %copy-start.26 = (f32[4,30]{1,0:T(4,128)S(1)}, f32[4,30]{1,0:T(4,128)}, u32[]{:S(2)}) copy-start(f32[4,30]{1,0:T(4,128)} %get-tuple-element.44) | copy-start | bytes 1444
  156.5 10.0 %copy-start.27 = (f32[1,1,512]{2,0,1:T(1,128)S(1)}, f32[1,1,512]{2,0,1:T(1,128)}, u32[]{:S(2)}) copy-start(f32[1,1,512]{2,0,1:T(1,128)} %get-tuple-element.34) | copy-start | bytes 6148
  156.5 10.0 %copy-start.28 = (f32[1,1,512]{2,0,1:T(1,128)S(1)}, f32[1,1,512]{2,0,1:T(1,128)}, u32[]{:S(2)}) copy-start(f32[1,1,512]{2,0,1:T(1,128)} %get-tuple-element.41) | copy-start | bytes 6148
  156.6 10.0 %copy-start.31 = (f32[1,1,512]{2,0,1:T(1,128)S(1)}, f32[1,1,512]{2,0,1:T(1,128)}, u32[]{:S(2)}) copy-start(f32[1,1,512]{2,0,1:T(1,128)} %get-tuple-element.22) | copy-start | bytes 6148
  156.6 10.0 %copy-start.32 = (f32[1,1,512]{2,0,1:T(1,128)S(1)}, f32[1,1,512]{2,0,1:T(1,128)}, u32[]{:S(2)}) copy-start(f32[1,1,512]{2,0,1:T(1,128)} %get-tuple-element.23) | copy-start | bytes 6148
  156.6 10.0 %copy-start.33 = (f32[1,1,512]{2,0,1:T(1,128)S(1)}, f32[1,1,512]{2,0,1:T(1,128)}, u32[]{:S(2)}) copy-start(f32[1,1,512]{2,0,1:T(1,128)} %get-tuple-element.31) | copy-start | bytes 6148
  156.6 10.0 %copy-start.34 = (f32[1,1,512]{2,0,1:T(1,128)S(1)}, f32[1,1,512]{2,0,1:T(1,128)}, u32[]{:S(2)}) copy-start(f32[1,1,512]{2,0,1:T(1,128)} %get-tuple-element.32) | copy-start | bytes 6148
  157.3 9.6 %copy-start.23 = (f32[4,30]{1,0:T(4,128)S(1)}, f32[4,30]{1,0:T(4,128)}, u32[]{:S(2)}) copy-start(f32[4,30]{1,0:T(4,128)} %get-tuple-element.42) | copy-start | bytes 1444
  157.3 9.6 %copy-start.24 = (f32[1,1,512]{2,0,1:T(1,128)S(1)}, f32[1,1,512]{2,0,1:T(1,128)}, u32[]{:S(2)}) copy-start(f32[1,1,512]{2,0,1:T(1,128)} %get-tuple-element.40) | copy-start | bytes 6148
  157.3 9.6 %copy-start.29 = (f32[1,1,512]{2,0,1:T(1,128)S(1)}, f32[1,1,512]{2,0,1:T(1,128)}, u32[]{:S(2)}) copy-start(f32[1,1,512]{2,0,1:T(1,128)} %get-tuple-element.15) | copy-start | bytes 6148
  157.3 11.1 %collective-permute-start = (bf16[1,30,8,512]{3,2,1,0:T(8,128)(2,1)S(1)}, bf16[1,30,8,512]{3,2,1,0:T(8,128)(2,1)S(1)}, u32[]{:S(2)}, u32[]{:S(2)}) collective-permute-start(bf16[1,30,8,512]{3,2,1,0:T(8,128)(2,1)S(1)} %get-tuple-element.13), channel_id=1, source_target_pairs={{0,8},{8,16},{16,24},{24,32},{32,40},{40,48},{48,56},{56,64},{64,7... | collective-permute-start | bytes 737288 | tf_op jit(solution)/shard_map/ppermute | solution.py:21
  159.3 11.0 %collective-permute-start.1 = (bf16[1,30,8,512]{3,2,1,0:T(8,128)(2,1)S(1)}, bf16[1,30,8,512]{3,2,1,0:T(8,128)(2,1)S(1)}, u32[]{:S(2)}, u32[]{:S(2)}) collective-permute-start(bf16[1,30,8,512]{3,2,1,0:T(8,128)(2,1)S(1)} %get-tuple-element.14), channel_id=1, source_target_pairs={{8,0},{16,8},{24,16},{32,24},{40,32},{48,40},{56,48},{64,56},{72,6... | collective-permute-start | bytes 737288 | tf_op jit(solution)/shard_map/ppermute | solution.py:22
  173.0 13.4 %copy-start.9 = (f32[4,30,512]{2,1,0:T(8,128)S(1)}, f32[4,30,512]{2,1,0:T(8,128)}, u32[]{:S(2)}) copy-start(f32[4,30,512]{2,1,0:T(8,128)} %get-tuple-element.70) | copy-start | bytes 737284
  173.0 13.4 %copy-start.10 = (f32[4,30,512]{2,1,0:T(8,128)S(1)}, f32[4,30,512]{2,1,0:T(8,128)}, u32[]{:S(2)}) copy-start(f32[4,30,512]{2,1,0:T(8,128)} %get-tuple-element.84) | copy-start | bytes 737284
  173.0 13.4 %copy-start.11 = (f32[4,30,512]{2,1,0:T(8,128)S(1)}, f32[4,30,512]{2,1,0:T(8,128)}, u32[]{:S(2)}) copy-start(f32[4,30,512]{2,1,0:T(8,128)} %get-tuple-element.58) | copy-start | bytes 737284
  173.0 13.4 %copy-start.12 = (f32[4,30,512]{2,1,0:T(8,128)S(1)}, f32[4,30,512]{2,1,0:T(8,128)}, u32[]{:S(2)}) copy-start(f32[4,30,512]{2,1,0:T(8,128)} %get-tuple-element.90) | copy-start | bytes 737284
  173.0 13.4 %copy-start.13 = (f32[4,30,512]{2,1,0:T(8,128)S(1)}, f32[4,30,512]{2,1,0:T(8,128)}, u32[]{:S(2)}) copy-start(f32[4,30,512]{2,1,0:T(8,128)} %get-tuple-element.64) | copy-start | bytes 737284
  173.1 13.4 %copy-start.14 = (f32[4,30,512]{2,1,0:T(8,128)S(1)}, f32[4,30,512]{2,1,0:T(8,128)}, u32[]{:S(2)}) copy-start(f32[4,30,512]{2,1,0:T(8,128)} %get-tuple-element.87) | copy-start | bytes 737284
  173.1 11.4 %collective-permute-start.2 = (bf16[1,30,8,512]{3,2,1,0:T(8,128)(2,1)S(1)}, bf16[1,30,8,512]{3,2,1,0:T(8,128)(2,1)S(1)}, u32[]{:S(2)}, u32[]{:S(2)}) collective-permute-start(bf16[1,30,8,512]{3,2,1,0:T(8,128)(2,1)S(1)} %get-tuple-element.11), channel_id=1, source_target_pairs={{0,8},{8,16},{16,24},{24,32},{32,40},{40,48},{48,56},{56,64},{64,7... | collective-permute-start | bytes 737288 | tf_op jit(solution)/shard_map/ppermute | solution.py:21
  175.2 11.1 %collective-permute-start.3 = (bf16[1,30,8,512]{3,2,1,0:T(8,128)(2,1)S(1)}, bf16[1,30,8,512]{3,2,1,0:T(8,128)(2,1)S(1)}, u32[]{:S(2)}, u32[]{:S(2)}) collective-permute-start(bf16[1,30,8,512]{3,2,1,0:T(8,128)(2,1)S(1)} %get-tuple-element.12), channel_id=1, source_target_pairs={{8,0},{16,8},{24,16},{32,24},{40,32},{48,40},{56,48},{64,56},{72,6... | collective-permute-start | bytes 737288 | tf_op jit(solution)/shard_map/ppermute | solution.py:22
  188.9 13.4 %copy-start.3 = (f32[4,30,512]{2,1,0:T(8,128)S(1)}, f32[4,30,512]{2,1,0:T(8,128)}, u32[]{:S(2)}) copy-start(f32[4,30,512]{2,1,0:T(8,128)} %get-tuple-element.69) | copy-start | bytes 737284
  188.9 13.4 %copy-start.4 = (f32[4,30,512]{2,1,0:T(8,128)S(1)}, f32[4,30,512]{2,1,0:T(8,128)}, u32[]{:S(2)}) copy-start(f32[4,30,512]{2,1,0:T(8,128)} %get-tuple-element.85) | copy-start | bytes 737284
  188.9 13.4 %copy-start.5 = (f32[4,30,512]{2,1,0:T(8,128)S(1)}, f32[4,30,512]{2,1,0:T(8,128)}, u32[]{:S(2)}) copy-start(f32[4,30,512]{2,1,0:T(8,128)} %get-tuple-element.57) | copy-start | bytes 737284
  188.9 13.4 %copy-start.6 = (f32[4,30,512]{2,1,0:T(8,128)S(1)}, f32[4,30,512]{2,1,0:T(8,128)}, u32[]{:S(2)}) copy-start(f32[4,30,512]{2,1,0:T(8,128)} %get-tuple-element.91) | copy-start | bytes 737284
  188.9 13.4 %copy-start.7 = (f32[4,30,512]{2,1,0:T(8,128)S(1)}, f32[4,30,512]{2,1,0:T(8,128)}, u32[]{:S(2)}) copy-start(f32[4,30,512]{2,1,0:T(8,128)} %get-tuple-element.63) | copy-start | bytes 737284
  188.9 13.4 %copy-start.8 = (f32[4,30,512]{2,1,0:T(8,128)S(1)}, f32[4,30,512]{2,1,0:T(8,128)}, u32[]{:S(2)}) copy-start(f32[4,30,512]{2,1,0:T(8,128)} %get-tuple-element.88) | copy-start | bytes 737284
  189.0 11.4 %collective-permute-start.4 = (bf16[1,30,8,512]{3,2,1,0:T(8,128)(2,1)S(1)}, bf16[1,30,8,512]{3,2,1,0:T(8,128)(2,1)S(1)}, u32[]{:S(2)}, u32[]{:S(2)}) collective-permute-start(bf16[1,30,8,512]{3,2,1,0:T(8,128)(2,1)S(1)} %get-tuple-element.9), channel_id=1, source_target_pairs={{0,8},{8,16},{16,24},{24,32},{32,40},{40,48},{48,56},{56,64},{64,7... | collective-permute-start | bytes 737288 | tf_op jit(solution)/shard_map/ppermute | solution.py:21
  191.0 11.1 %collective-permute-start.5 = (bf16[1,30,8,512]{3,2,1,0:T(8,128)(2,1)S(1)}, bf16[1,30,8,512]{3,2,1,0:T(8,128)(2,1)S(1)}, u32[]{:S(2)}, u32[]{:S(2)}) collective-permute-start(bf16[1,30,8,512]{3,2,1,0:T(8,128)(2,1)S(1)} %get-tuple-element.10), channel_id=1, source_target_pairs={{8,0},{16,8},{24,16},{32,24},{40,32},{48,40},{56,48},{64,56},{72,6... | collective-permute-start | bytes 737288 | tf_op jit(solution)/shard_map/ppermute | solution.py:22
  (14 other events, 62.5 us)
Sparse Core Ops, SparseCore 0:
  10.0 64.7 all-gather.4
  76.9 61.5 all-gather.2
where the time goes:
time: 213 us; the launch traced here: 212 us
  waiting for transfers between devices  121 us (57%)
  starting transfers between devices  28.2 us (13%)
  matrix products  21.7 us (10%)
  local copies, waits for them, and re-layouts  20 us (9%)
  between operations  14.2 us (7%)
  other arithmetic  6.81 us (3%)
    all_gather x1, waiting for transfers between devices, local(): piece_keys = lax.all_gather(key_rows, 'chan', axis=1, tiled=True)  56 us
    all_gather x1, waiting for transfers between devices, local(): piece_values = lax.all_gather(value_rows, 'chan', axis=1, tiled=True)  54.7 us
    ppermute x3, starting transfers between devices, with_halo(): after = lax.ppermute(leading, axis, down)  22.1 us
    dot_general x1, matrix products, online_update(): jnp.einsum('flgrn,fngd->flgrd', weights, value_heads, precision=lax.Preci...  9.51 us
    dot_general x3, matrix products, clear_layer(): jnp.dot(mixed_term.reshape(-1, mixed_term.shape[-1]), w_mix, preferred_el...  7.93 us
    ppermute x3, starting transfers between devices, with_halo(): before = lax.ppermute(last, axis, up)  6.02 us
    reshape x1, local copies, waits for them, and re-layouts, online_update(): value_rows.astype(jnp.float32)  5.58 us
    ppermute x3, waiting for transfers between devices, with_halo(): before = lax.ppermute(last, axis, up)  5.32 us
  transfers between devices with their start and end apart: 8, of which 8 were waited for; matrix products, arithmetic and copies ran while one was open for 8% of the time, Pallas kernels for 0%

commit v1 on v0

v1 whole, which is shorter than its diff:
```python
import functools

import jax
import jax.numpy as jnp
from jax import lax
from jax.experimental import pallas as pl
from jax.experimental.pallas import tpu as pltpu
from jax.sharding import PartitionSpec as P

HEADS = 8
HEAD_DIM = 64
NBLK = 72
LAYERS = 3
NX, NY = 4, 2
CHAN = NX * NY
LINES, SCAN = 4, 30
PER = LINES * SCAN // CHAN
ROWS = 16
BLK = NBLK // CHAN
LAT, D, CB = 64, 512, 128
LG = LAT // CHAN
CHUNKS = 3
PC = PER // CHUNKS
MASKED = -1e30
MESH = pl.DeviceIdType.MESH
OFFSETS = ((2, 1), (2, 0), (1, 1), (3, 1), (1, 0), (3, 0), (0, 1))


def nt_dot(a, b):
    return lax.dot_general(a, b, (((1,), (1,)), ((), ())), preferred_element_type=jnp.float32)


def kernel(
    tracks, rad, wk, wv, q, bb, cnt, vm, w_out, taps, w_mix, out,
    xf, kv_send, kv_recv, kf, vf, qbt, bias, att, lsend, lrecv, grid_f, tb, st, hsend, hrecv,
    kv_ssem, kv_rsem, l_ssem, l_rsem, h_ssem, h_rsem, own_sem,
):
    track, me = lax.axis_index("track"), lax.axis_index("chan")
    x, y = me // NY, me % NY
    up, down = (track + tracks - 1) % tracks, (track + 1) % tracks

    def to_peer(o):
        return ((x + o[0]) % NX) * NY + (y + o[1]) % NY

    def from_peer(o):
        return ((x + NX - o[0]) % NX) * NY + (y + NY - o[1]) % NY

    barrier = pltpu.get_barrier_semaphore()
    for o in OFFSETS:
        pl.semaphore_signal(barrier, inc=1, device_id=(track, to_peer(o)), device_id_type=MESH)
    for other in (up, down):
        pl.semaphore_signal(barrier, inc=1, device_id=(other, me), device_id_type=MESH)

    xf[pl.ds(SCAN * BLK * LINES, 72), :] = jnp.zeros((72, CB), jnp.float32)
    xf[pl.ds(0, SCAN * BLK * LINES), :] = (
        rad[...].astype(jnp.float32).reshape(SCAN * BLK * LINES, CB)
    )

    for b in range(BLK):
        rows = jnp.concatenate(
            [
                xf[pl.ds((j % 2) * BLK * LINES + b * LINES + j // 2, ROWS, stride=2 * BLK * LINES), :]
                for j in range(CHAN)
            ],
            axis=0,
        )
        inverse = lax.rsqrt(jnp.mean(rows * rows, axis=-1, keepdims=True) + 1e-05)
        normed = (rows * inverse).astype(jnp.bfloat16)
        keys = jnp.dot(rows.astype(jnp.bfloat16), wk[b], preferred_element_type=jnp.float32)
        values = jnp.dot(normed, wv[b], preferred_element_type=jnp.float32)
        kv_send[:, 0, b] = keys.astype(jnp.bfloat16).reshape(CHAN, ROWS, CB)
        kv_send[:, 1, b] = values.astype(jnp.bfloat16).reshape(CHAN, ROWS, CB)

    pl.semaphore_wait(barrier, len(OFFSETS) + 2)

    def kv_copy(o, i):
        return pltpu.make_async_remote_copy(
            src_ref=kv_send.at[to_peer(o)],
            dst_ref=kv_recv.at[me],
            send_sem=kv_ssem.at[i],
            recv_sem=kv_rsem.at[i],
            device_id=(track, to_peer(o)),
            device_id_type=MESH,
        )

    for i, o in enumerate(OFFSETS):
        kv_copy(o, i).start()

    lane = lax.broadcasted_iota(jnp.int32, (LAT, CB), 1)
    low = lane < HEAD_DIM
    for h in range(HEADS):
        e = h // 4
        part = q[:, (h // 2) * CB : (h // 2 + 1) * CB].astype(jnp.float32) * HEAD_DIM**-0.5
        if h % 2 != e:
            part = pltpu.roll(part, HEAD_DIM, 1)
        part = jnp.where(low if e == 0 else jnp.logical_not(low), part, 0.0)
        qbt[h * LAT : (h + 1) * LAT, :] = part.astype(jnp.bfloat16)

    group = lax.broadcasted_iota(jnp.int32, (CHAN, 48), 0)
    slot = lax.broadcasted_iota(jnp.int32, (CHAN, 48), 1)
    used = jnp.zeros((CHAN, 48), jnp.int32)
    for g in range(CHAN):
        used = jnp.where(group == g, cnt[g], used)
    blocks = jnp.where(slot < used, bb[...], -1)
    block_of = lax.broadcasted_iota(jnp.int32, (CHAN, CB), 1)
    allowed = jnp.full((CHAN, CB), MASKED, jnp.float32)
    for j in range(48):
        allowed = jnp.where(blocks[:, j : j + 1] == block_of, 0.0, allowed)
    for g in range(CHAN):
        bias[g * LG : (g + 1) * LG, :] = jnp.broadcast_to(allowed[g : g + 1], (LG, CB))

    for c in range(LAYERS):
        for k in range(9):
            tb[c * 9 + k] = jnp.broadcast_to(taps[k, c : c + 1], (LG, D))
    for s in range(2):
        for edge in (0, SCAN + 1):
            grid_f[s, :, edge] = jnp.zeros((LINES + 2, LG, D), jnp.float32)
    kf[pl.ds(NBLK * ROWS, (CB - NBLK) * ROWS), :] = jnp.zeros(((CB - NBLK) * ROWS, CB), jnp.float32)
    vf[pl.ds(NBLK * ROWS, (CB - NBLK) * ROWS), :] = jnp.zeros(((CB - NBLK) * ROWS, CB), jnp.float32)

    def spread(ref, s):
        at = pl.ds(pl.multiple_of(s * (BLK * ROWS), BLK * ROWS), BLK * ROWS)
        kf[at, :] = ref[s, 0].astype(jnp.float32).reshape(BLK * ROWS, CB)
        vf[at, :] = ref[s, 1].astype(jnp.float32).reshape(BLK * ROWS, CB)

    spread(kv_send, me)
    for i in reversed(range(len(OFFSETS))):
        o = OFFSETS[i]
        kv_copy(o, i).wait_recv()
        spread(kv_recv, from_peer(o))

    line_me, side_me = me // 2, me % 2

    def lat_copy(o, i, c):
        return pltpu.make_async_remote_copy(
            src_ref=lsend.at[to_peer(o), pl.ds(c * PC, PC)],
            dst_ref=lrecv.at[line_me, pl.ds(c * PC, PC), side_me],
            send_sem=l_ssem.at[c, i],
            recv_sem=l_rsem.at[c, i],
            device_id=(track, to_peer(o)),
            device_id_type=MESH,
        )

    def own_copy(c):
        return pltpu.make_async_copy(
            lsend.at[me, pl.ds(c * PC, PC)],
            lrecv.at[line_me, pl.ds(c * PC, PC), side_me],
            own_sem.at[c],
        )

    ones = jnp.ones((CB, CB), jnp.bfloat16)
    low_v = lax.broadcasted_iota(jnp.int32, (CB, CB), 1) < HEAD_DIM
    for c in range(CHUNKS):

        def attend(mm, _):
            m = c * PC + mm
            keys = kf[pl.ds(m, CB, stride=ROWS), :].astype(jnp.bfloat16)
            values = vf[pl.ds(m, CB, stride=ROWS), :]
            swapped = pltpu.roll(values, HEAD_DIM, 1)
            scores = nt_dot(qbt[...], keys).reshape(HEADS, LAT, CB) + bias[...][None]
            peak = jnp.max(scores, axis=-1, keepdims=True)
            weights = jnp.exp(scores - peak).astype(jnp.bfloat16)
            for e in range(2):
                pair = jnp.where(low_v, values, swapped) if e == 0 else jnp.where(low_v, swapped, values)
                both = jnp.concatenate([pair.astype(jnp.bfloat16), ones], axis=1)
                sums = jnp.dot(
                    weights[e * 4 : (e + 1) * 4].reshape(4 * LAT, CB), both,
                    preferred_element_type=jnp.float32,
                )
                for t in range(2):
                    a, b = sums[2 * t * LAT : (2 * t + 1) * LAT], sums[(2 * t + 1) * LAT : (2 * t + 2) * LAT]
                    top = jnp.where(low, a[:, :CB], b[:, :CB])
                    bottom = jnp.where(low, a[:, CB:], b[:, CB:])
                    at = (e * 2 + t) * CB
                    att[mm, :, at : at + CB] = (top / bottom).astype(jnp.bfloat16)
            return 0

        lax.fori_loop(0, PC, attend, 0)
        mixed = jnp.dot(
            att[...].reshape(PC * LAT, D), w_out[...], preferred_element_type=jnp.float32
        ).reshape(PC, LAT, D)
        latents = (q[...].astype(jnp.float32)[None] + mixed).reshape(PC, CHAN, LG, D)
        for g in range(CHAN):
            lsend[g, c * PC : (c + 1) * PC] = latents[:, g].astype(jnp.bfloat16)
        for i, o in enumerate(OFFSETS):
            lat_copy(o, i, c).start()
        own_copy(c).start()

    for c in range(CHUNKS):
        own_copy(c).wait()
        for i, o in enumerate(OFFSETS):
            src = from_peer(o)
            pltpu.make_async_remote_copy(
                src_ref=lsend.at[0, pl.ds(c * PC, PC)],
                dst_ref=lrecv.at[src // 2, pl.ds(c * PC, PC), src % 2],
                send_sem=l_ssem.at[c, i],
                recv_sem=l_rsem.at[c, i],
                device_id=(track, to_peer(o)),
                device_id_type=MESH,
            ).wait_recv()

    def halo_copy(c, way):
        return pltpu.make_async_remote_copy(
            src_ref=hsend.at[c, way],
            dst_ref=hrecv.at[c, way],
            send_sem=h_ssem.at[c, way],
            recv_sem=h_rsem.at[c, way],
            device_id=((up, down)[way], me),
            device_id_type=MESH,
        )

    for way, l in ((0, 0), (1, LINES - 1)):
        hsend[0, way] = lrecv[l].reshape(SCAN, LG, D)
        halo_copy(0, way).start()
    for l in range(LINES):
        grid_f[0, l + 1, 1 : SCAN + 1] = lrecv[l].reshape(SCAN, LG, D).astype(jnp.float32)

    for c in range(LAYERS):
        now, later = c % 2, (c + 1) % 2

        def clear_line(l):
            def column(i, _):
                for dp in range(2):
                    p = 2 * i + dp
                    scale = [vm[k, l, p].astype(jnp.float32) for k in range(9)]
                    for f in range(D // CB):
                        lanes = slice(f * CB, (f + 1) * CB)
                        total = None
                        for k in range(9):
                            term = (scale[k] * tb[c * 9 + k, :, lanes]) * grid_f[
                                now, l + k // 3, p + k % 3, :, lanes
                            ]
                            total = term if total is None else total + term
                        st[p, :, lanes] = total.astype(jnp.bfloat16)
                return 0

            lax.fori_loop(0, SCAN // 2, column, 0)
            update = jnp.dot(
                st[...].reshape(SCAN * LG, D), w_mix[c], preferred_element_type=jnp.float32
            ).reshape(SCAN, LG, D)
            return (grid_f[now, l + 1, 1 : SCAN + 1] + update).astype(jnp.bfloat16)

        def keep(l, cleared):
            if c == LAYERS - 1:
                out[l] = cleared
            else:
                grid_f[later, l + 1, 1 : SCAN + 1] = cleared.astype(jnp.float32)

        for l in range(1, LINES - 1):
            keep(l, clear_line(l))
        for way, edge, outside in ((1, 0, 0), (0, LINES + 1, tracks - 1)):
            halo_copy(c, way).wait_recv()
            beside = hrecv[c, way].astype(jnp.float32)
            grid_f[now, edge, 1 : SCAN + 1] = jnp.where(track == outside, 0.0, beside)
        for way, l in ((0, 0), (1, LINES - 1)):
            cleared = clear_line(l)
            keep(l, cleared)
            if c < LAYERS - 1:
                hsend[c + 1, way] = cleared
                halo_copy(c + 1, way).start()

    for i, o in enumerate(OFFSETS):
        kv_copy(o, i).wait_send()
        for c in range(CHUNKS):
            lat_copy(o, i, c).wait_send()
    for c in range(LAYERS):
        for way in range(2):
            halo_copy(c, way).wait_send()


def local(tracks, radiance, w_key, w_value, latent_query, band_blocks, band_count, valid_mask, w_out, conv_taps, w_mix):
    vmem = pl.BlockSpec(memory_space=pltpu.VMEM)
    smem = pl.BlockSpec(memory_space=pltpu.SMEM)
    bf16, f32 = jnp.bfloat16, jnp.float32
    dma = pltpu.SemaphoreType.DMA
    peers = len(OFFSETS)
    return pl.pallas_call(
        functools.partial(kernel, tracks),
        out_shape=jax.ShapeDtypeStruct((LINES, SCAN, LG, D), bf16),
        in_specs=[vmem, vmem, vmem, vmem, vmem, smem, smem, vmem, vmem, vmem],
        out_specs=vmem,
        scratch_shapes=[
            pltpu.VMEM((SCAN * BLK * LINES + 72, CB), f32),
            pltpu.VMEM((CHAN, 2, BLK, ROWS, CB), bf16),
            pltpu.VMEM((CHAN, 2, BLK, ROWS, CB), bf16),
            pltpu.VMEM((CB * ROWS, CB), f32),
            pltpu.VMEM((CB * ROWS, CB), f32),
            pltpu.VMEM((HEADS * LAT, CB), bf16),
            pltpu.VMEM((LAT, CB), f32),
            pltpu.VMEM((PC, LAT, D), bf16),
            pltpu.VMEM((CHAN, PER, LG, D), bf16),
            pltpu.VMEM((LINES, PER, 2, LG, D), bf16),
            pltpu.VMEM((2, LINES + 2, SCAN + 2, LG, D), f32),
            pltpu.VMEM((LAYERS * 9, LG, D), f32),
            pltpu.VMEM((SCAN, LG, D), bf16),
            pltpu.VMEM((LAYERS, 2, SCAN, LG, D), bf16),
            pltpu.VMEM((LAYERS, 2, SCAN, LG, D), bf16),
            dma((peers,)), dma((peers,)),
            dma((CHUNKS, peers)), dma((CHUNKS, peers)),
            dma((LAYERS, 2)), dma((LAYERS, 2)),
            dma((CHUNKS,)),
        ],
        compiler_params=pltpu.CompilerParams(
            collective_id=0, has_side_effects=True, vmem_limit_bytes=60 * 1024 * 1024
        ),
    )(
        jnp.transpose(radiance, (1, 2, 0, 3)), w_key, w_value, latent_query, band_blocks, band_count,
        jnp.transpose(valid_mask, (2, 0, 1)), w_out, jnp.transpose(conv_taps, (1, 0, 2)), w_mix,
    )


def solution(mesh):
    return jax.shard_map(
        functools.partial(local, mesh.shape["track"]),
        mesh=mesh,
        in_specs=(
            P("track", None, "chan", None),
            P("chan", None, None),
            P("chan", None, None),
            P(),
            P(),
            P(),
            P("track", None, None),
            P(),
            P(),
            P(),
        ),
        out_specs=P("track", None, "chan", None),
        check_vma=False,
    )
```

time: 213 us -> 66.5 us (0.31)
  the two profiles are of different devices: /device:TPU:24 before, /device:TPU:4 now
where the time goes in v1:
time: 66.5 us; the launch traced here: 66.3 us
  Pallas kernels  64.1 us (96%)
  local copies, waits for them, and re-layouts  2.21 us (3%)
    pallas_call x1, Pallas kernels, local(): pl.pallas_call(functools.partial(kernel, tracks), out_shape=jax.ShapeDtyp...  64.1 us
    unnamed x1, local copies, waits for them, and re-layouts  2.21 us

profile of v1, /device:TPU:4, one launch (start us, length us, event | category | flops | bytes accessed | tf_op | source)
XLA Modules:
  0.0 66.3 jit_solution(5179139860084344261)
XLA Ops:
  0.0 64.1 %shard_map.100 = bf16[4,30,8,512]{3,2,1,0:T(8,128)(2,1)} custom-call(bf16[30,9,4,128]{3,2,1,0:T(4,128)(2,1)} %bitcast.3, bf16[9,128,128]{2,1,0:T(8,128)(2,1)} %wk.1, bf16[9,128,128]{2,1,0:T(8,128)(2,1)} %wv.1, bf16[64,512]{1,0:T(8,128)(2,1)} %q.1, s32[8,48]{1,0:T(8,128)} %bb.1, s32[8]{0:T(128)} %cnt.1, s32[9,4,30]{2,1,0:T(4,128)} %bitcast.5, ...), custom_call_target="tpu_custom_call" | custom-call | tf_op jit(solution)/shard_map/pallas_call | solution.py:277
  64.1 2.2 %copy.12 = bf16[4,30,8,512]{3,2,1,0:T(8,128)(2,1)} copy(bf16[4,30,8,512]{3,2,1,0:T(8,128)(2,1)} %shard_map.100) | data formatting | bytes 1966080

commit v2 on v1

v2 whole, which is shorter than its diff:
```python
import functools

import jax
import jax.numpy as jnp
from jax import lax
from jax.experimental import pallas as pl
from jax.experimental.pallas import tpu as pltpu
from jax.sharding import PartitionSpec as P

HEADS = 8
HEAD_DIM = 64
NBLK = 72
LAYERS = 3
NX, NY = 4, 2
CHAN = NX * NY
LINES, SCAN = 4, 30
WIDE = 32
PER = LINES * SCAN // CHAN
ROWS = 16
BLK = NBLK // CHAN
LAT, D, CB = 64, 512, 128
FT = D // CB
LG = LAT // CHAN
MAXB = 48
HALF = LG // 2
STEP = 4
CHUNKS = ROWS // STEP
MASKED = -1e30
MESH = pl.DeviceIdType.MESH
OFFSETS = ((2, 1), (2, 0), (1, 1), (3, 1), (1, 0), (3, 0), (0, 1))
BF16, F32 = jnp.bfloat16, jnp.float32


def nt_dot(a, b):
    return lax.dot_general(a, b, (((1,), (1,)), ((), ())), preferred_element_type=F32)


def chunk_at(c):
    return pl.ds(c * STEP, min(STEP, PER - c * STEP))


def kernel(
    tracks, rad_h, wk_h, wv_h, q_h, bb_h, cnt_h, vm_h, w_out_h, taps_h, w_mix_h, out_h,
    rad, wk, wv, q, bb, cnt, vm, w_out, taps, w_mix,
    xf, kv_send, kv_recv, kf, vf, qbt, bias, att, lsend, lrecv, near,
    vmf, mb, coef, turn, grid_f, st, hsend, hrecv, last, outb,
    in_sem, kv_ssem, kv_rsem, l_ssem, l_rsem, n_ssem, n_rsem, h_ssem, h_rsem, out_sem,
):
    track, me = lax.axis_index("track"), lax.axis_index("chan")
    x, y = me // NY, me % NY
    up, down = (track + tracks - 1) % tracks, (track + 1) % tracks
    ways = (up, down)

    def to_peer(o):
        return ((x + o[0]) % NX) * NY + (y + o[1]) % NY

    def from_peer(o):
        return ((x + NX - o[0]) % NX) * NY + (y + NY - o[1]) % NY

    barrier = pltpu.get_barrier_semaphore()
    for o in OFFSETS:
        pl.semaphore_signal(barrier, inc=1, device_id=(track, to_peer(o)), device_id_type=MESH)
    for other in ways:
        pl.semaphore_signal(barrier, inc=1, device_id=(other, me), device_id_type=MESH)

    loads = [
        pltpu.make_async_copy(src, dst, in_sem.at[i])
        for i, (src, dst) in enumerate(
            (
                (rad_h, rad), (wk_h, wk), (wv_h, wv), (q_h, q), (bb_h, bb), (cnt_h, cnt),
                (vm_h, vm), (taps_h, taps), (w_out_h, w_out), (w_mix_h, w_mix),
            )
        )
    ]
    for load in loads:
        load.start()

    xf[pl.ds(SCAN * BLK * LINES, 72), :] = jnp.zeros((72, CB), F32)
    loads[0].wait()
    xf[pl.ds(0, SCAN * BLK * LINES), :] = rad[...].astype(F32).reshape(SCAN * BLK * LINES, CB)
    loads[1].wait()
    loads[2].wait()

    for b in range(BLK):
        rows = jnp.concatenate(
            [
                xf[pl.ds((j % 2) * BLK * LINES + b * LINES + j // 2, ROWS, stride=2 * BLK * LINES), :]
                for j in range(CHAN)
            ],
            axis=0,
        )
        inverse = lax.rsqrt(jnp.mean(rows * rows, axis=-1, keepdims=True) + 1e-05)
        normed = (rows * inverse).astype(BF16)
        keys = jnp.dot(rows.astype(BF16), wk[b], preferred_element_type=F32)
        values = jnp.dot(normed, wv[b], preferred_element_type=F32)
        kv_send[:, :, 0, b] = keys.astype(BF16).reshape(CHAN, 2, 8, CB)
        kv_send[:, :, 1, b] = values.astype(BF16).reshape(CHAN, 2, 8, CB)

    pl.semaphore_wait(barrier, len(OFFSETS) + 2)

    def kv_copy(o, i, c):
        return pltpu.make_async_remote_copy(
            src_ref=kv_send.at[to_peer(o), c],
            dst_ref=kv_recv.at[me, c],
            send_sem=kv_ssem.at[c, i],
            recv_sem=kv_rsem.at[c, i],
            device_id=(track, to_peer(o)),
            device_id_type=MESH,
        )

    for c in range(2):
        for i, o in enumerate(OFFSETS):
            kv_copy(o, i, c).start()

    for load in loads[3:]:
        load.wait()
    lane = lax.broadcasted_iota(jnp.int32, (LAT, CB), 1)
    low = lane < HEAD_DIM
    for h in range(HEADS):
        e = h // 4
        part = q[:, (h // 2) * CB : (h // 2 + 1) * CB].astype(F32) * HEAD_DIM**-0.5
        if h % 2 != e:
            part = pltpu.roll(part, HEAD_DIM, 1)
        part = jnp.where(low if e == 0 else jnp.logical_not(low), part, 0.0)
        qbt[h * LAT : (h + 1) * LAT, :] = part.astype(BF16)

    group = lax.broadcasted_iota(jnp.int32, (CHAN, MAXB), 0)
    slot = lax.broadcasted_iota(jnp.int32, (CHAN, MAXB), 1)
    used = jnp.zeros((CHAN, MAXB), jnp.int32)
    for g in range(CHAN):
        used = jnp.where(group == g, cnt[g], used)
    blocks = jnp.where(slot < used, bb[...], -1)
    block_of = lax.broadcasted_iota(jnp.int32, (CHAN, CB), 1)
    allowed = jnp.full((CHAN, CB), MASKED, F32)
    for j in range(MAXB):
        allowed = jnp.where(blocks[:, j : j + 1] == block_of, 0.0, allowed)
    for g in range(CHAN):
        bias[g * LG : (g + 1) * LG, :] = jnp.broadcast_to(allowed[g : g + 1], (LG, CB))

    kf[:, pl.ds(NBLK * 8, (CB - NBLK) * 8), :] = jnp.zeros((2, (CB - NBLK) * 8, CB), F32)
    vf[:, pl.ds(NBLK * 8, (CB - NBLK) * 8), :] = jnp.zeros((2, (CB - NBLK) * 8, CB), F32)

    def spread(ref, s, c):
        at = pl.ds(pl.multiple_of(s * (BLK * 8), BLK * 8), BLK * 8)
        kf[c, at, :] = ref[s, c, 0].astype(F32).reshape(BLK * 8, CB)
        vf[c, at, :] = ref[s, c, 1].astype(F32).reshape(BLK * 8, CB)

    for c in range(2):
        spread(kv_send, me, c)

    vmf[...] = jnp.zeros((CB, CB), F32)
    for k in range(9):
        vmf[k * LINES : (k + 1) * LINES, 0:SCAN] = vm[k].astype(F32)
    turned = vmf[...].T
    for l in range(LINES):
        for k in range(9):
            col = turned[:WIDE, k * LINES + l : k * LINES + l + 1]
            mb[l, k] = jnp.broadcast_to(col, (WIDE, CB))

    def coefficients(l, _):
        for c in range(LAYERS):
            for f in range(FT):
                for k in range(9):
                    coef[c, l, f, k] = mb[l, k] * taps[k, c : c + 1, f * CB : (f + 1) * CB]
        return 0

    lax.fori_loop(0, LINES, coefficients, 0)

    def borders(l, _):
        for s in range(2):
            for i in range(LG):
                grid_f[s, l, i, :, 0:8] = jnp.zeros((FT, 8, CB), F32)
                grid_f[s, l, i, :, 8 + WIDE : 16 + WIDE] = jnp.zeros((FT, 8, CB), F32)
        turn[l, :, SCAN * LG : WIDE * LG] = jnp.zeros((FT, (WIDE - SCAN) * LG, CB), F32)
        return 0

    lax.fori_loop(0, LINES + 2, borders, 0)

    line_me, side_me = me // 2, me % 2

    def lat_copy(o, i, c):
        return pltpu.make_async_remote_copy(
            src_ref=lsend.at[to_peer(o), chunk_at(c)],
            dst_ref=lrecv.at[line_me, chunk_at(c), side_me],
            send_sem=l_ssem.at[c, i],
            recv_sem=l_rsem.at[c, me],
            device_id=(track, to_peer(o)),
            device_id_type=MESH,
        )

    def own_copy(c):
        return pltpu.make_async_copy(
            lsend.at[me, chunk_at(c)],
            lrecv.at[line_me, chunk_at(c), side_me],
            l_rsem.at[c, me],
        )

    def await_latents(s, c):
        pltpu.make_async_copy(
            lsend.at[s, chunk_at(c)], lrecv.at[s // 2, chunk_at(c), s % 2], l_rsem.at[c, s]
        ).wait()

    def near_copy(c, way):
        return pltpu.make_async_remote_copy(
            src_ref=lrecv.at[way * (LINES - 1), chunk_at(c)],
            dst_ref=near.at[way, chunk_at(c)],
            send_sem=n_ssem.at[c, way],
            recv_sem=n_rsem.at[c, way],
            device_id=(ways[way], me),
            device_id_type=MESH,
        )

    def forward(c):
        for way in range(2):
            for s in range(2):
                await_latents(way * (CHAN - 2) + s, c)
            near_copy(c, way).start()

    ones = jnp.ones((CB, CB), BF16)
    low_v = lax.broadcasted_iota(jnp.int32, (CB, CB), 1) < HEAD_DIM

    def attend(c, n):
        def some(pair, _):
            tags = [(mm, e) for mm in range(n) for e in range(2)]
            at = [c % 2 * STEP + pair * n + mm for mm in range(n)]
            keys = [kf[c // 2, pl.ds(a, CB, stride=8), :].astype(BF16) for a in at]
            values = [vf[c // 2, pl.ds(a, CB, stride=8), :] for a in at]
            swapped = [pltpu.roll(v, HEAD_DIM, 1) for v in values]
            both = {
                (mm, e): jnp.concatenate(
                    [
                        (
                            jnp.where(low_v, values[mm], swapped[mm])
                            if e == 0
                            else jnp.where(low_v, swapped[mm], values[mm])
                        ).astype(BF16),
                        ones,
                    ],
                    axis=1,
                )
                for mm, e in tags
            }
            scores = {
                (mm, e): nt_dot(qbt[e * 4 * LAT : (e + 1) * 4 * LAT, :], keys[mm]).reshape(4, LAT, CB)
                + bias[...][None]
                for mm, e in tags
            }
            peaks = {t: jnp.max(scores[t], axis=-1, keepdims=True) for t in tags}
            weights = {t: jnp.exp(scores[t] - peaks[t]).astype(BF16) for t in tags}
            for mm, e in tags:
                sums = jnp.dot(
                    weights[mm, e].reshape(4 * LAT, CB), both[mm, e], preferred_element_type=F32
                )
                for t in range(2):
                    a = sums[2 * t * LAT : (2 * t + 1) * LAT]
                    b = sums[(2 * t + 1) * LAT : (2 * t + 2) * LAT]
                    top = jnp.where(low, a[:, :CB], b[:, :CB])
                    bottom = jnp.where(low, a[:, CB:], b[:, CB:])
                    lanes = (e * 2 + t) * CB
                    att[pair * n + mm, :, lanes : lanes + CB] = (top / bottom).astype(BF16)
            return 0

        lax.fori_loop(0, STEP // n, some, 0)
        mixed = jnp.dot(
            att[...].reshape(STEP * LAT, D), w_out[...], preferred_element_type=F32
        ).reshape(STEP, LAT, D)
        latents = (q[...].astype(F32)[None] + mixed).reshape(STEP, CHAN, LG, D)
        for g in range(CHAN):
            lsend[g, c * STEP : (c + 1) * STEP] = latents[:, g].astype(BF16)
        for i, o in enumerate(OFFSETS):
            lat_copy(o, i, c).start()
        own_copy(c).start()

    for c in range(CHUNKS):
        if c % 2 == 0:
            for i in reversed(range(len(OFFSETS))):
                o = OFFSETS[i]
                kv_copy(o, i, c // 2).wait_recv()
                spread(kv_recv, from_peer(o), c // 2)
        attend(c, 2)
        if c >= 2:
            forward(c - 2)
    for c in range(CHUNKS - 2, CHUNKS):
        forward(c)

    def regrid(source, l):
        for f in range(FT):
            turn[l, f, 0 : SCAN * LG] = source[:, :, f * CB : (f + 1) * CB].reshape(SCAN * LG, CB)
        for i in range(LG):
            for f in range(FT):
                grid_f[0, l, i, f, 8 : 8 + WIDE] = turn[l, f, pl.ds(i, WIDE, stride=LG), :]

    for c in range(CHUNKS):
        for s in range(2, CHAN - 2):
            await_latents(s, c)
    for l in range(LINES):
        regrid(lrecv[l].reshape(SCAN, LG, D).astype(F32), l + 1)

    def halo_copy(c, half, way):
        return pltpu.make_async_remote_copy(
            src_ref=hsend.at[c, half, way],
            dst_ref=hrecv.at[c, half, way],
            send_sem=h_ssem.at[c, half, way],
            recv_sem=h_rsem.at[c, half, way],
            device_id=(ways[way], me),
            device_id_type=MESH,
        )

    beyond = (tracks - 1, 0)
    edge_line = (LINES + 1, 0)

    def out_copy(l):
        return pltpu.make_async_copy(outb.at[l], out_h.at[l], out_sem.at[l])

    for c in range(LAYERS):
        now, later = c % 2, (c + 1) % 2
        final = c == LAYERS - 1

        def clear_pair(half, first, apart):
            def line(n, _):
                l = first + n * apart
                for f in range(FT):
                    for t in range(WIDE // 8):
                        cs = [coef[c, l, f, k, 8 * t : 8 * t + 8] for k in range(9)]
                        for i in range(HALF):
                            total = None
                            for k in range(9):
                                term = cs[k] * grid_f[
                                    now, l + k // 3, half * HALF + i, f, pl.ds(7 + 8 * t + k % 3, 8), :
                                ]
                                total = term if total is None else total + term
                            st[n, i, 8 * t : 8 * t + 8, f * CB : (f + 1) * CB] = total.astype(BF16)
                return 0

            lax.fori_loop(0, 2, line, 0)
            update = jnp.dot(
                st[...].reshape(2 * HALF * WIDE, D), w_mix[c], preferred_element_type=F32
            ).reshape(2, HALF, WIDE, D)
            for n in range(2):
                l = first + n * apart
                for i in range(HALF):
                    for f in range(FT):
                        lanes = slice(f * CB, (f + 1) * CB)
                        centre = grid_f[now, l + 1, half * HALF + i, f, 8 : 8 + WIDE]
                        cleared = (centre + update[n, i, :, lanes]).astype(BF16)
                        if final:
                            at = (half * HALF + i) * WIDE
                            last[l, f, at : at + WIDE] = cleared.astype(F32)
                        else:
                            grid_f[later, l + 1, half * HALF + i, f, 8 : 8 + WIDE] = cleared.astype(F32)
                            if apart > 1:
                                hsend[c, half, n, i, :, lanes] = cleared

        def finish_pair(first, apart):
            def column(p, _):
                for n in range(2):
                    for f in range(FT):
                        rows = last[first + n * apart, f, pl.ds(p, LG, stride=WIDE), :]
                        outb[first + n * apart, p, :, f * CB : (f + 1) * CB] = rows.astype(BF16)
                return 0

            lax.fori_loop(0, SCAN, column, 0)
            for n in range(2):
                out_copy(first + n * apart).start()

        for half in range(2):
            clear_pair(half, 1, 1)
        if final:
            finish_pair(1, 1)
        for half in range(2):
            for way in range(2):
                if c == 0:
                    if half == 0:
                        for n in range(CHUNKS):
                            near_copy(n, way).wait_recv()
                        beside = near[way].reshape(SCAN, LG, D).astype(F32)
                        regrid(jnp.where(track == beyond[way], 0.0, beside), edge_line[way])
                else:
                    halo_copy(c - 1, half, way).wait_recv()
                    for i in range(HALF):
                        for f in range(FT):
                            beside = hrecv[c - 1, half, way, i, :, f * CB : (f + 1) * CB].astype(F32)
                            grid_f[now, edge_line[way], half * HALF + i, f, 8 : 8 + WIDE] = jnp.where(
                                track == beyond[way], 0.0, beside
                            )
            clear_pair(half, 0, LINES - 1)
            if not final:
                for way in range(2):
                    halo_copy(c, half, way).start()
    finish_pair(0, LINES - 1)

    for i, o in enumerate(OFFSETS):
        for c in range(2):
            kv_copy(o, i, c).wait_send()
        for c in range(CHUNKS):
            lat_copy(o, i, c).wait_send()
    for way in range(2):
        for c in range(CHUNKS):
            near_copy(c, way).wait_send()
        for c in range(LAYERS - 1):
            for half in range(2):
                halo_copy(c, half, way).wait_send()
    for l in range(LINES):
        out_copy(l).wait()


def local(tracks, radiance, w_key, w_value, latent_query, band_blocks, band_count, valid_mask, w_out, conv_taps, w_mix):
    hbm = pl.BlockSpec(memory_space=pl.ANY)
    vmem = pltpu.VMEM
    dma = pltpu.SemaphoreType.DMA
    peers = len(OFFSETS)
    return pl.pallas_call(
        functools.partial(kernel, tracks),
        out_shape=jax.ShapeDtypeStruct((LINES, SCAN, LG, D), BF16),
        in_specs=[hbm] * 10,
        out_specs=hbm,
        scratch_shapes=[
            vmem((SCAN, BLK, LINES, CB), BF16),
            vmem((BLK, CB, CB), BF16),
            vmem((BLK, CB, CB), BF16),
            vmem((LAT, D), BF16),
            vmem((CHAN, MAXB), jnp.int32),
            pltpu.SMEM((CHAN,), jnp.int32),
            vmem((9, LINES, SCAN), jnp.int32),
            vmem((D, D), BF16),
            vmem((9, LAYERS, D), F32),
            vmem((LAYERS, D, D), BF16),
            vmem((SCAN * BLK * LINES + 72, CB), F32),
            vmem((CHAN, 2, 2, BLK, 8, CB), BF16),
            vmem((CHAN, 2, 2, BLK, 8, CB), BF16),
            vmem((2, CB * 8, CB), F32),
            vmem((2, CB * 8, CB), F32),
            vmem((HEADS * LAT, CB), BF16),
            vmem((LAT, CB), F32),
            vmem((STEP, LAT, D), BF16),
            vmem((CHAN, ROWS, LG, D), BF16),
            vmem((LINES, PER, 2, LG, D), BF16),
            vmem((2, PER, 2, LG, D), BF16),
            vmem((CB, CB), F32),
            vmem((LINES, 9, WIDE, CB), F32),
            vmem((LAYERS, LINES, FT, 9, WIDE, CB), F32),
            vmem((LINES + 2, FT, WIDE * LG, CB), F32),
            vmem((2, LINES + 2, LG, FT, WIDE + 16, CB), F32),
            vmem((2, HALF, WIDE, D), BF16),
            vmem((LAYERS - 1, 2, 2, HALF, WIDE, D), BF16),
            vmem((LAYERS - 1, 2, 2, HALF, WIDE, D), BF16),
            vmem((LINES, FT, LG * WIDE, CB), F32),
            vmem((LINES, SCAN, LG, D), BF16),
            dma((10,)),
            dma((2, peers)), dma((2, peers)),
            dma((CHUNKS, peers)), dma((CHUNKS, CHAN)),
            dma((CHUNKS, 2)), dma((CHUNKS, 2)),
            dma((LAYERS - 1, 2, 2)), dma((LAYERS - 1, 2, 2)),
            dma((LINES,)),
        ],
        compiler_params=pltpu.CompilerParams(
            collective_id=0, has_side_effects=True, vmem_limit_bytes=60 * 1024 * 1024
        ),
    )(
        jnp.transpose(radiance, (1, 2, 0, 3)), w_key, w_value, latent_query, band_blocks, band_count,
        jnp.transpose(valid_mask, (2, 0, 1)), w_out, jnp.transpose(conv_taps, (1, 0, 2)), w_mix,
    )


def solution(mesh):
    return jax.shard_map(
        functools.partial(local, mesh.shape["track"]),
        mesh=mesh,
        in_specs=(
            P("track", None, "chan", None),
            P("chan", None, None),
            P("chan", None, None),
            P(),
            P(),
            P(),
            P("track", None, None),
            P(),
            P(),
            P(),
        ),
        out_specs=P("track", None, "chan", None),
        check_vma=False,
    )
```

time: 66.5 us -> 58.7 us (0.88)
  the two profiles are of different devices: /device:TPU:4 before, /device:TPU:8 now
where the time goes in v2:
time: 58.7 us; the launch traced here: 58.5 us
  Pallas kernels  56.3 us (96%)
  local copies, waits for them, and re-layouts  2.21 us (4%)
    pallas_call x1, Pallas kernels, local(): pl.pallas_call(functools.partial(kernel, tracks), out_shape=jax.ShapeDtyp...  56.3 us
    unnamed x1, local copies, waits for them, and re-layouts  2.21 us

profile of v2, /device:TPU:8, one launch (start us, length us, event | category | flops | bytes accessed | tf_op | source)
XLA Modules:
  0.0 58.5 jit_solution(7172654096094055950)
XLA Ops:
  0.0 56.3 %shard_map.100 = bf16[4,30,8,512]{3,2,1,0:T(8,128)(2,1)} custom-call(bf16[30,9,4,128]{3,2,1,0:T(4,128)(2,1)} %bitcast.3, bf16[9,128,128]{2,1,0:T(8,128)(2,1)} %wk_h.1, bf16[9,128,128]{2,1,0:T(8,128)(2,1)} %wv_h.1, bf16[64,512]{1,0:T(8,128)(2,1)} %q_h.1, s32[8,48]{1,0:T(8,128)} %bb_h.1, s32[8]{0:T(128)} %cnt_h.1, s32[9,4,30]{2,1,0:T(4,128)} %bitcast.5, ...), custom_call_target="tpu_custom_call" | custom-call | tf_op jit(solution)/shard_map/pallas_call | solution.py:412
  56.3 2.2 %copy.12 = bf16[4,30,8,512]{3,2,1,0:T(8,128)(2,1)} copy(bf16[4,30,8,512]{3,2,1,0:T(8,128)(2,1)} %shard_map.100) | data formatting | bytes 1966080

commit v3 on v2

--- a/solution.py
+++ b/solution.py
@@ -11,6 +11,7 @@
 HEAD_DIM = 64
 NBLK = 72
 LAYERS = 3
+DEEP = 2
 NX, NY = 4, 2
 CHAN = NX * NY
 LINES, SCAN = 4, 30
@@ -25,6 +26,9 @@
 HALF = LG // 2
 STEP = 4
 CHUNKS = ROWS // STEP
+EXCH = max(LAYERS - DEEP, 1)
+ALL = LINES + 2 * DEEP
+CLEAR = ALL - 2
 MASKED = -1e30
 MESH = pl.DeviceIdType.MESH
 OFFSETS = ((2, 1), (2, 0), (1, 1), (3, 1), (1, 0), (3, 0), (0, 1))
@@ -41,15 +45,17 @@
 
 def kernel(
     tracks, rad_h, wk_h, wv_h, q_h, bb_h, cnt_h, vm_h, w_out_h, taps_h, w_mix_h, out_h,
-    rad, wk, wv, q, bb, cnt, vm, w_out, taps, w_mix,
+    rad, wk, wv, q, bb, cnt, vm, w_out, taps, w_mix, vm_near,
     xf, kv_send, kv_recv, kf, vf, qbt, bias, att, lsend, lrecv, near,
     vmf, mb, coef, turn, grid_f, st, hsend, hrecv, last, outb,
-    in_sem, kv_ssem, kv_rsem, l_ssem, l_rsem, n_ssem, n_rsem, h_ssem, h_rsem, out_sem,
+    in_sem, kv_ssem, kv_rsem, l_ssem, l_rsem, n_ssem, n_rsem, v_ssem, v_rsem, h_ssem, h_rsem, out_sem,
 ):
     track, me = lax.axis_index("track"), lax.axis_index("chan")
     x, y = me // NY, me % NY
     up, down = (track + tracks - 1) % tracks, (track + 1) % tracks
     ways = (up, down)
+    not_first, not_last = track > 0, track < tracks - 1
+    sends, comes = (not_first, not_last), (not_last, not_first)
 
     def to_peer(o):
         return ((x + o[0]) % NX) * NY + (y + o[1]) % NY
@@ -60,8 +66,11 @@
     barrier = pltpu.get_barrier_semaphore()
     for o in OFFSETS:
         pl.semaphore_signal(barrier, inc=1, device_id=(track, to_peer(o)), device_id_type=MESH)
-    for other in ways:
-        pl.semaphore_signal(barrier, inc=1, device_id=(other, me), device_id_type=MESH)
+    for way in range(2):
+
+        @pl.when(sends[way])
+        def _():
+            pl.semaphore_signal(barrier, inc=1, device_id=(ways[way], me), device_id_type=MESH)
 
     loads = [
         pltpu.make_async_copy(src, dst, in_sem.at[i])
@@ -96,7 +105,7 @@
         kv_send[:, :, 0, b] = keys.astype(BF16).reshape(CHAN, 2, 8, CB)
         kv_send[:, :, 1, b] = values.astype(BF16).reshape(CHAN, 2, 8, CB)
 
-    pl.semaphore_wait(barrier, len(OFFSETS) + 2)
+    pl.semaphore_wait(barrier, len(OFFSETS) + not_first.astype(jnp.int32) + not_last.astype(jnp.int32))
 
     def kv_copy(o, i, c):
         return pltpu.make_async_remote_copy(
@@ -114,6 +123,23 @@
 
     for load in loads[3:]:
         load.wait()
+
+    def vm_copy(way):
+        return pltpu.make_async_remote_copy(
+            src_ref=vm,
+            dst_ref=vm_near.at[way],
+            send_sem=v_ssem.at[way],
+            recv_sem=v_rsem.at[way],
+            device_id=(ways[way], me),
+            device_id_type=MESH,
+        )
+
+    for way in range(2):
+
+        @pl.when(sends[way])
+        def _():
+            vm_copy(way).start()
+
     lane = lax.broadcasted_iota(jnp.int32, (LAT, CB), 1)
     low = lane < HEAD_DIM
     for h in range(HEADS):
@@ -148,14 +174,33 @@
     for c in range(2):
         spread(kv_send, me, c)
 
-    vmf[...] = jnp.zeros((CB, CB), F32)
-    for k in range(9):
-        vmf[k * LINES : (k + 1) * LINES, 0:SCAN] = vm[k].astype(F32)
-    turned = vmf[...].T
-    for l in range(LINES):
+    def validity(slot, source, lines):
+        vmf[slot] = jnp.zeros((CB, CB), F32)
         for k in range(9):
-            col = turned[:WIDE, k * LINES + l : k * LINES + l + 1]
-            mb[l, k] = jnp.broadcast_to(col, (WIDE, CB))
+            vmf[slot, k * LINES : (k + 1) * LINES, 0:SCAN] = source(k).astype(F32)
+        turned = vmf[slot].T
+        for l, to in lines:
+            for k in range(9):
+                col = turned[:WIDE, k * LINES + l : k * LINES + l + 1]
+                mb[to, k] = jnp.broadcast_to(col, (WIDE, CB))
+
+    validity(0, lambda k: vm[k], [(l, l + DEEP - 1) for l in range(LINES)])
+    for way in range(2):
+
+        @pl.when(comes[way])
+        def _():
+            vm_copy(way).wait_recv()
+
+            if way == 0:
+                lines = [(l, DEEP - 1 + LINES + l) for l in range(DEEP - 1)]
+            else:
+                lines = [(LINES - DEEP + 1 + l, l) for l in range(DEEP - 1)]
+            validity(1 + way, lambda k: vm_near[way, k], lines)
+
+        @pl.when(jnp.logical_not(comes[way]))
+        def _():
+            for l in range(DEEP - 1):
+                mb[l if way == 1 else DEEP - 1 + LINES + l] = jnp.zeros((9, WIDE, CB), F32)
 
     def coefficients(l, _):
         for c in range(LAYERS):
@@ -164,7 +209,7 @@
                     coef[c, l, f, k] = mb[l, k] * taps[k, c : c + 1, f * CB : (f + 1) * CB]
         return 0
 
-    lax.fori_loop(0, LINES, coefficients, 0)
+    lax.fori_loop(0, CLEAR, coefficients, 0)
 
     def borders(l, _):
         for s in range(2):
@@ -174,7 +219,7 @@
         turn[l, :, SCAN * LG : WIDE * LG] = jnp.zeros((FT, (WIDE - SCAN) * LG, CB), F32)
         return 0
 
-    lax.fori_loop(0, LINES + 2, borders, 0)
+    lax.fori_loop(0, ALL, borders, 0)
 
     line_me, side_me = me // 2, me % 2
 
@@ -202,8 +247,8 @@
 
     def near_copy(c, way):
         return pltpu.make_async_remote_copy(
-            src_ref=lrecv.at[way * (LINES - 1), chunk_at(c)],
-            dst_ref=near.at[way, chunk_at(c)],
+            src_ref=lrecv.at[pl.ds(way * (LINES - DEEP), DEEP), chunk_at(c)],
+            dst_ref=near.at[way, :, chunk_at(c)],
             send_sem=n_ssem.at[c, way],
             recv_sem=n_rsem.at[c, way],
             device_id=(ways[way], me),
@@ -211,10 +256,14 @@
         )
 
     def forward(c):
+        for s in range(CHAN):
+            if s // 2 < DEEP or s // 2 >= LINES - DEEP:
+                await_latents(s, c)
         for way in range(2):
-            for s in range(2):
-                await_latents(way * (CHAN - 2) + s, c)
-            near_copy(c, way).start()
+
+            @pl.when(sends[way])
+            def _():
+                near_copy(c, way).start()
 
     ones = jnp.ones((CB, CB), BF16)
     low_v = lax.broadcasted_iota(jnp.int32, (CB, CB), 1) < HEAD_DIM
@@ -291,102 +340,143 @@
                 grid_f[0, l, i, f, 8 : 8 + WIDE] = turn[l, f, pl.ds(i, WIDE, stride=LG), :]
 
     for c in range(CHUNKS):
-        for s in range(2, CHAN - 2):
-            await_latents(s, c)
+        for s in range(CHAN):
+            if not (s // 2 < DEEP or s // 2 >= LINES - DEEP):
+                await_latents(s, c)
     for l in range(LINES):
-        regrid(lrecv[l].reshape(SCAN, LG, D).astype(F32), l + 1)
+        regrid(lrecv[l].reshape(SCAN, LG, D).astype(F32), l + DEEP)
 
     def halo_copy(c, half, way):
         return pltpu.make_async_remote_copy(
-            src_ref=hsend.at[c, half, way],
-            dst_ref=hrecv.at[c, half, way],
-            send_sem=h_ssem.at[c, half, way],
-            recv_sem=h_rsem.at[c, half, way],
+            src_ref=hsend.at[c - DEEP, half, way],
+            dst_ref=hrecv.at[c - DEEP, half, way],
+            send_sem=h_ssem.at[c - DEEP, half, way],
+            recv_sem=h_rsem.at[c - DEEP, half, way],
             device_id=(ways[way], me),
             device_id_type=MESH,
         )
 
-    beyond = (tracks - 1, 0)
-    edge_line = (LINES + 1, 0)
-
     def out_copy(l):
         return pltpu.make_async_copy(outb.at[l], out_h.at[l], out_sem.at[l])
 
-    for c in range(LAYERS):
+    def clear_pair(c, half, out):
         now, later = c % 2, (c + 1) % 2
+        apart = CLEAR - 1 - 2 * out
+        own = out - DEEP + 1
         final = c == LAYERS - 1
 
-        def clear_pair(half, first, apart):
-            def line(n, _):
-                l = first + n * apart
+        def line(n, _):
+            l = out + n * apart
+            for f in range(FT):
+                for t in range(WIDE // 8):
+                    cs = [coef[c, l, f, k, 8 * t : 8 * t + 8] for k in range(9)]
+                    for i in range(HALF):
+                        total = None
+                        for k in range(9):
+                            term = cs[k] * grid_f[
+                                now, l + k // 3, half * HALF + i, f, pl.ds(7 + 8 * t + k % 3, 8), :
+                            ]
+                            total = term if total is None else total + term
+                        st[n, i, 8 * t : 8 * t + 8, f * CB : (f + 1) * CB] = total.astype(BF16)
+            return 0
+
+        lax.fori_loop(0, 2, line, 0)
+        update = jnp.dot(
+            st[...].reshape(2 * HALF * WIDE, D), w_mix[c], preferred_element_type=F32
+        ).reshape(2, HALF, WIDE, D)
+        for n in range(2):
+            l = out + n * apart
+            for i in range(HALF):
                 for f in range(FT):
-                    for t in range(WIDE // 8):
-                        cs = [coef[c, l, f, k, 8 * t : 8 * t + 8] for k in range(9)]
-                        for i in range(HALF):
-                            total = None
-                            for k in range(9):
-                                term = cs[k] * grid_f[
-                                    now, l + k // 3, half * HALF + i, f, pl.ds(7 + 8 * t + k % 3, 8), :
-                                ]
-                                total = term if total is None else total + term
-                            st[n, i, 8 * t : 8 * t + 8, f * CB : (f + 1) * CB] = total.astype(BF16)
-                return 0
-
-            lax.fori_loop(0, 2, line, 0)
-            update = jnp.dot(
-                st[...].reshape(2 * HALF * WIDE, D), w_mix[c], preferred_element_type=F32
-            ).reshape(2, HALF, WIDE, D)
+                    lanes = slice(f * CB, (f + 1) * CB)
+                    centre = grid_f[now, l + 1, half * HALF + i, f, 8 : 8 + WIDE]
+                    cleared = (centre + update[n, i, :, lanes]).astype(BF16)
+                    wide = cleared.astype(F32)
+                    if final:
+                        at = (half * HALF + i) * WIDE
+                        last[l - DEEP + 1, f, at : at + WIDE] = wide
+                    else:
+                        if own < 0:
+                            wide = jnp.where(comes[1 - n], wide, 0.0)
+                        grid_f[later, l + 1, half * HALF + i, f, 8 : 8 + WIDE] = wide
+                        if own == 0 and c + 1 >= DEEP:
+                            hsend[c + 1 - DEEP, half, n, i, :, lanes] = cleared
+        if own == 0 and not final and c + 1 >= DEEP:
+            for way in range(2):
+
+                @pl.when(sends[way])
+                def _():
+                    halo_copy(c + 1, half, way).start()
+
+    def finish_pair(first, apart):
+        def column(p, _):
             for n in range(2):
-                l = first + n * apart
-                for i in range(HALF):
-                    for f in range(FT):
-                        lanes = slice(f * CB, (f + 1) * CB)
-                        centre = grid_f[now, l + 1, half * HALF + i, f, 8 : 8 + WIDE]
-                        cleared = (centre + update[n, i, :, lanes]).astype(BF16)
-                        if final:
-                            at = (half * HALF + i) * WIDE
-                            last[l, f, at : at + WIDE] = cleared.astype(F32)
-                        else:
-                            grid_f[later, l + 1, half * HALF + i, f, 8 : 8 + WIDE] = cleared.astype(F32)
-                            if apart > 1:
-                                hsend[c, half, n, i, :, lanes] = cleared
-
-        def finish_pair(first, apart):
-            def column(p, _):
-                for n in range(2):
-                    for f in range(FT):
-                        rows = last[first + n * apart, f, pl.ds(p, LG, stride=WIDE), :]
-                        outb[first + n * apart, p, :, f * CB : (f + 1) * CB] = rows.astype(BF16)
-                return 0
-
-            lax.fori_loop(0, SCAN, column, 0)
-            for n in range(2):
-                out_copy(first + n * apart).start()
-
+                for f in range(FT):
+                    rows = last[first + n * apart, f, pl.ds(p, LG, stride=WIDE), :]
+                    outb[first + n * apart, p, :, f * CB : (f + 1) * CB] = rows.astype(BF16)
+            return 0
+
+        lax.fori_loop(0, SCAN, column, 0)
+        for n in range(2):
+            out_copy(first + n * apart).start()
+
+    def take_near():
+        for way in range(2):
+            base = (DEEP + LINES, 0)[way]
+
+            @pl.when(comes[way])
+            def _():
+                for n in range(CHUNKS):
+                    near_copy(n, way).wait_recv()
+                for d in range(DEEP):
+                    regrid(near[way, d].reshape(SCAN, LG, D).astype(F32), base + d)
+
+            @pl.when(jnp.logical_not(comes[way]))
+            def _():
+                for d in range(DEEP):
+                    for i in range(LG):
+                        grid_f[0, base + d, i, :, 8 : 8 + WIDE] = jnp.zeros((FT, WIDE, CB), F32)
+
+    def take_halo(c, half, way):
+        edge = (DEEP + LINES, DEEP - 1)[way]
+        own = pl.ds(half * HALF, HALF)
+
+        @pl.when(comes[way])
+        def _():
+            halo_copy(c, half, way).wait_recv()
+            for f in range(FT):
+                grid_f[c % 2, edge, own, f, 8 : 8 + WIDE] = hrecv[
+                    c - DEEP, half, way, :, :, f * CB : (f + 1) * CB
+                ].astype(F32)
+
+        @pl.when(jnp.logical_not(comes[way]))
+        def _():
+            for f in range(FT):
+                grid_f[c % 2, edge, own, f, 8 : 8 + WIDE] = jnp.zeros((HALF, WIDE, CB), F32)
+
+    inner, outer = DEEP, DEEP - 1
+    for half in range(2):
+        clear_pair(0, half, inner)
+    take_near()
+    for out in range(outer, -1, -1):
         for half in range(2):
-            clear_pair(half, 1, 1)
-        if final:
-            finish_pair(1, 1)
-        for half in range(2):
-            for way in range(2):
-                if c == 0:
-                    if half == 0:
-                        for n in range(CHUNKS):
-                            near_copy(n, way).wait_recv()
-                        beside = near[way].reshape(SCAN, LG, D).astype(F32)
-                        regrid(jnp.where(track == beyond[way], 0.0, beside), edge_line[way])
-                else:
-                    halo_copy(c - 1, half, way).wait_recv()
-                    for i in range(HALF):
-                        for f in range(FT):
-                            beside = hrecv[c - 1, half, way, i, :, f * CB : (f + 1) * CB].astype(F32)
-                            grid_f[now, edge_line[way], half * HALF + i, f, 8 : 8 + WIDE] = jnp.where(
-                                track == beyond[way], 0.0, beside
-                            )
-            clear_pair(half, 0, LINES - 1)
-            if not final:
+            clear_pair(0, half, out)
+    for c in range(1, LAYERS):
+        if c < DEEP:
+            for out in range(c, DEEP + 1):
+                for half in range(2):
+                    clear_pair(c, half, out)
+                if out == inner and c == LAYERS - 1:
+                    finish_pair(1, 1)
+        else:
+            for half in range(2):
+                clear_pair(c, half, inner)
+            if c == LAYERS - 1:
+                finish_pair(1, 1)
+            for half in range(2):
                 for way in range(2):
-                    halo_copy(c, half, way).start()
+                    take_halo(c, half, way)
+                clear_pair(c, half, outer)
     finish_pair(0, LINES - 1)
 
     for i, o in enumerate(OFFSETS):
@@ -395,11 +485,16 @@
         for c in range(CHUNKS):
             lat_copy(o, i, c).wait_send()
     for way in range(2):
-        for c in range(CHUNKS):
-            near_copy(c, way).wait_send()
-        for c in range(LAYERS - 1):
-            for half in range(2):
-                halo_copy(c, half, way).wait_send()
+
+        @pl.when(sends[way])
+        def _():
+            vm_copy(way).wait_send()
+            for c in range(CHUNKS):
+                near_copy(c, way).wait_send()
+            for c in range(DEEP, LAYERS):
+                for half in range(2):
+                    halo_copy(c, half, way).wait_send()
+
     for l in range(LINES):
         out_copy(l).wait()
 
@@ -425,6 +520,7 @@
             vmem((D, D), BF16),
             vmem((9, LAYERS, D), F32),
             vmem((LAYERS, D, D), BF16),
+            vmem((2, 9, LINES, SCAN), jnp.int32),
             vmem((SCAN * BLK * LINES + 72, CB), F32),
             vmem((CHAN, 2, 2, BLK, 8, CB), BF16),
             vmem((CHAN, 2, 2, BLK, 8, CB), BF16),
@@ -435,22 +531,23 @@
             vmem((STEP, LAT, D), BF16),
             vmem((CHAN, ROWS, LG, D), BF16),
             vmem((LINES, PER, 2, LG, D), BF16),
-            vmem((2, PER, 2, LG, D), BF16),
-            vmem((CB, CB), F32),
-            vmem((LINES, 9, WIDE, CB), F32),
-            vmem((LAYERS, LINES, FT, 9, WIDE, CB), F32),
-            vmem((LINES + 2, FT, WIDE * LG, CB), F32),
-            vmem((2, LINES + 2, LG, FT, WIDE + 16, CB), F32),
+            vmem((2, DEEP, PER, 2, LG, D), BF16),
+            vmem((3, CB, CB), F32),
+            vmem((CLEAR, 9, WIDE, CB), F32),
+            vmem((LAYERS, CLEAR, FT, 9, WIDE, CB), F32),
+            vmem((ALL, FT, WIDE * LG, CB), F32),
+            vmem((2, ALL, LG, FT, WIDE + 16, CB), F32),
             vmem((2, HALF, WIDE, D), BF16),
-            vmem((LAYERS - 1, 2, 2, HALF, WIDE, D), BF16),
-            vmem((LAYERS - 1, 2, 2, HALF, WIDE, D), BF16),
+            vmem((EXCH, 2, 2, HALF, WIDE, D), BF16),
+            vmem((EXCH, 2, 2, HALF, WIDE, D), BF16),
             vmem((LINES, FT, LG * WIDE, CB), F32),
             vmem((LINES, SCAN, LG, D), BF16),
             dma((10,)),
             dma((2, peers)), dma((2, peers)),
             dma((CHUNKS, peers)), dma((CHUNKS, CHAN)),
             dma((CHUNKS, 2)), dma((CHUNKS, 2)),
-            dma((LAYERS - 1, 2, 2)), dma((LAYERS - 1, 2, 2)),
+            dma((2,)), dma((2,)),
+            dma((EXCH, 2, 2)), dma((EXCH, 2, 2)),
             dma((LINES,)),
         ],
         compiler_params=pltpu.CompilerParams(

time: 58.7 us -> 53.3 us (0.908)
  the two profiles are of different devices: /device:TPU:8 before, /device:TPU:24 now
where the time goes in v3:
time: 53.3 us; the launch traced here: 52.8 us
  Pallas kernels  50.6 us (95%)
  local copies, waits for them, and re-layouts  2.21 us (4%)
    pallas_call x1, Pallas kernels, local(): pl.pallas_call(functools.partial(kernel, tracks), out_shape=jax.ShapeDtyp...  50.6 us
    unnamed x1, local copies, waits for them, and re-layouts  2.21 us

profile of v3, /device:TPU:24, one launch (start us, length us, event | category | flops | bytes accessed | tf_op | source)
XLA Modules:
  0.0 52.8 jit_solution(2497912745048394335)
XLA Ops:
  0.0 50.6 %shard_map.100 = bf16[4,30,8,512]{3,2,1,0:T(8,128)(2,1)} custom-call(bf16[30,9,4,128]{3,2,1,0:T(4,128)(2,1)} %bitcast.3, bf16[9,128,128]{2,1,0:T(8,128)(2,1)} %wk_h.1, bf16[9,128,128]{2,1,0:T(8,128)(2,1)} %wv_h.1, bf16[64,512]{1,0:T(8,128)(2,1)} %q_h.1, s32[8,48]{1,0:T(8,128)} %bb_h.1, s32[8]{0:T(128)} %cnt_h.1, s32[9,4,30]{2,1,0:T(4,128)} %bitcast.5, ...), custom_call_target="tpu_custom_call" | custom-call | tf_op jit(solution)/shard_map/pallas_call | solution.py:507
  50.6 2.2 %copy.12 = bf16[4,30,8,512]{3,2,1,0:T(8,128)(2,1)} copy(bf16[4,30,8,512]{3,2,1,0:T(8,128)(2,1)} %shard_map.100) | data formatting | bytes 1966080

commit v4 on v3

--- a/solution.py
+++ b/solution.py
@@ -93,7 +93,7 @@
     for b in range(BLK):
         rows = jnp.concatenate(
             [
-                xf[pl.ds((j % 2) * BLK * LINES + b * LINES + j // 2, ROWS, stride=2 * BLK * LINES), :]
+                xf[pl.ds((j % 2) * PER * BLK * LINES + b * LINES + j // 2, ROWS, stride=BLK * LINES), :]
                 for j in range(CHAN)
             ],
             axis=0,
@@ -102,8 +102,8 @@
         normed = (rows * inverse).astype(BF16)
         keys = jnp.dot(rows.astype(BF16), wk[b], preferred_element_type=F32)
         values = jnp.dot(normed, wv[b], preferred_element_type=F32)
-        kv_send[:, :, 0, b] = keys.astype(BF16).reshape(CHAN, 2, 8, CB)
-        kv_send[:, :, 1, b] = values.astype(BF16).reshape(CHAN, 2, 8, CB)
+        kv_send[:, :, 0, b] = keys.astype(BF16).reshape(CHAN, CHUNKS, STEP, CB)
+        kv_send[:, :, 1, b] = values.astype(BF16).reshape(CHAN, CHUNKS, STEP, CB)
 
     pl.semaphore_wait(barrier, len(OFFSETS) + not_first.astype(jnp.int32) + not_last.astype(jnp.int32))
 
@@ -117,7 +117,7 @@
             device_id_type=MESH,
         )
 
-    for c in range(2):
+    for c in range(CHUNKS):
         for i, o in enumerate(OFFSETS):
             kv_copy(o, i, c).start()
 
@@ -163,15 +163,15 @@
     for g in range(CHAN):
         bias[g * LG : (g + 1) * LG, :] = jnp.broadcast_to(allowed[g : g + 1], (LG, CB))
 
-    kf[:, pl.ds(NBLK * 8, (CB - NBLK) * 8), :] = jnp.zeros((2, (CB - NBLK) * 8, CB), F32)
-    vf[:, pl.ds(NBLK * 8, (CB - NBLK) * 8), :] = jnp.zeros((2, (CB - NBLK) * 8, CB), F32)
+    kf[:, pl.ds(NBLK * STEP, (CB - NBLK) * STEP), :] = jnp.zeros((CHUNKS, (CB - NBLK) * STEP, CB), F32)
+    vf[:, pl.ds(NBLK * STEP, (CB - NBLK) * STEP), :] = jnp.zeros((CHUNKS, (CB - NBLK) * STEP, CB), F32)
 
     def spread(ref, s, c):
-        at = pl.ds(pl.multiple_of(s * (BLK * 8), BLK * 8), BLK * 8)
-        kf[c, at, :] = ref[s, c, 0].astype(F32).reshape(BLK * 8, CB)
-        vf[c, at, :] = ref[s, c, 1].astype(F32).reshape(BLK * 8, CB)
-
-    for c in range(2):
+        at = pl.ds(s * (BLK * STEP), BLK * STEP)
+        kf[c, at, :] = ref[s, c, 0].astype(F32).reshape(BLK * STEP, CB)
+        vf[c, at, :] = ref[s, c, 1].astype(F32).reshape(BLK * STEP, CB)
+
+    for c in range(CHUNKS):
         spread(kv_send, me, c)
 
     def validity(slot, source, lines):
@@ -226,7 +226,7 @@
     def lat_copy(o, i, c):
         return pltpu.make_async_remote_copy(
             src_ref=lsend.at[to_peer(o), chunk_at(c)],
-            dst_ref=lrecv.at[line_me, chunk_at(c), side_me],
+            dst_ref=lrecv.at[line_me, side_me, chunk_at(c)],
             send_sem=l_ssem.at[c, i],
             recv_sem=l_rsem.at[c, me],
             device_id=(track, to_peer(o)),
@@ -236,19 +236,19 @@
     def own_copy(c):
         return pltpu.make_async_copy(
             lsend.at[me, chunk_at(c)],
-            lrecv.at[line_me, chunk_at(c), side_me],
+            lrecv.at[line_me, side_me, chunk_at(c)],
             l_rsem.at[c, me],
         )
 
     def await_latents(s, c):
         pltpu.make_async_copy(
-            lsend.at[s, chunk_at(c)], lrecv.at[s // 2, chunk_at(c), s % 2], l_rsem.at[c, s]
+            lsend.at[s, chunk_at(c)], lrecv.at[s // 2, s % 2, chunk_at(c)], l_rsem.at[c, s]
         ).wait()
 
     def near_copy(c, way):
         return pltpu.make_async_remote_copy(
-            src_ref=lrecv.at[pl.ds(way * (LINES - DEEP), DEEP), chunk_at(c)],
-            dst_ref=near.at[way, :, chunk_at(c)],
+            src_ref=lrecv.at[pl.ds(way * (LINES - DEEP), DEEP), :, chunk_at(c)],
+            dst_ref=near.at[way, :, :, chunk_at(c)],
             send_sem=n_ssem.at[c, way],
             recv_sem=n_rsem.at[c, way],
             device_id=(ways[way], me),
@@ -271,9 +271,9 @@
     def attend(c, n):
         def some(pair, _):
             tags = [(mm, e) for mm in range(n) for e in range(2)]
-            at = [c % 2 * STEP + pair * n + mm for mm in range(n)]
-            keys = [kf[c // 2, pl.ds(a, CB, stride=8), :].astype(BF16) for a in at]
-            values = [vf[c // 2, pl.ds(a, CB, stride=8), :] for a in at]
+            at = [pair * n + mm for mm in range(n)]
+            keys = [kf[c, pl.ds(a, CB, stride=STEP), :].astype(BF16) for a in at]
+            values = [vf[c, pl.ds(a, CB, stride=STEP), :] for a in at]
             swapped = [pltpu.roll(v, HEAD_DIM, 1) for v in values]
             both = {
                 (mm, e): jnp.concatenate(
@@ -321,11 +321,10 @@
         own_copy(c).start()
 
     for c in range(CHUNKS):
-        if c % 2 == 0:
-            for i in reversed(range(len(OFFSETS))):
-                o = OFFSETS[i]
-                kv_copy(o, i, c // 2).wait_recv()
-                spread(kv_recv, from_peer(o), c // 2)
+        for i in reversed(range(len(OFFSETS))):
+            o = OFFSETS[i]
+            kv_copy(o, i, c).wait_recv()
+            spread(kv_recv, from_peer(o), c)
         attend(c, 2)
         if c >= 2:
             forward(c - 2)
@@ -365,7 +364,7 @@
         own = out - DEEP + 1
         final = c == LAYERS - 1
 
-        def line(n, _):
+        def stencil(n):
             l = out + n * apart
             for f in range(FT):
                 for t in range(WIDE // 8):
@@ -378,29 +377,35 @@
                             ]
                             total = term if total is None else total + term
                         st[n, i, 8 * t : 8 * t + 8, f * CB : (f + 1) * CB] = total.astype(BF16)
-            return 0
-
-        lax.fori_loop(0, 2, line, 0)
-        update = jnp.dot(
-            st[...].reshape(2 * HALF * WIDE, D), w_mix[c], preferred_element_type=F32
-        ).reshape(2, HALF, WIDE, D)
-        for n in range(2):
+
+        def finish(n, update):
             l = out + n * apart
             for i in range(HALF):
                 for f in range(FT):
                     lanes = slice(f * CB, (f + 1) * CB)
                     centre = grid_f[now, l + 1, half * HALF + i, f, 8 : 8 + WIDE]
-                    cleared = (centre + update[n, i, :, lanes]).astype(BF16)
+                    cleared = (centre + update[i, :, lanes]).astype(BF16)
                     wide = cleared.astype(F32)
                     if final:
-                        at = (half * HALF + i) * WIDE
-                        last[l - DEEP + 1, f, at : at + WIDE] = wide
+                        at = pl.ds(pl.multiple_of((half * HALF + i) * WIDE, WIDE), WIDE)
+                        last[l - DEEP + 1, f, at] = wide
                     else:
                         if own < 0:
                             wide = jnp.where(comes[1 - n], wide, 0.0)
                         grid_f[later, l + 1, half * HALF + i, f, 8 : 8 + WIDE] = wide
                         if own == 0 and c + 1 >= DEEP:
                             hsend[c + 1 - DEEP, half, n, i, :, lanes] = cleared
+
+        def mix(n):
+            return jnp.dot(
+                st[n].reshape(HALF * WIDE, D), w_mix[c], preferred_element_type=F32
+            ).reshape(HALF, WIDE, D)
+
+        stencil(0)
+        first = mix(0)
+        stencil(1)
+        finish(0, first)
+        finish(1, mix(1))
         if own == 0 and not final and c + 1 >= DEEP:
             for way in range(2):
 
@@ -455,34 +460,43 @@
                 grid_f[c % 2, edge, own, f, 8 : 8 + WIDE] = jnp.zeros((HALF, WIDE, CB), F32)
 
     inner, outer = DEEP, DEEP - 1
-    for half in range(2):
-        clear_pair(0, half, inner)
+
+    def clear_both(c, out):
+        def one(half, _):
+            clear_pair(c, half, out)
+            return 0
+
+        lax.fori_loop(0, 2, one, 0)
+
+    def clear_with_halo(c):
+        def one(half, _):
+            for way in range(2):
+                take_halo(c, half, way)
+            clear_pair(c, half, outer)
+            return 0
+
+        lax.fori_loop(0, 2, one, 0)
+
+    clear_both(0, inner)
     take_near()
     for out in range(outer, -1, -1):
-        for half in range(2):
-            clear_pair(0, half, out)
+        clear_both(0, out)
     for c in range(1, LAYERS):
         if c < DEEP:
             for out in range(c, DEEP + 1):
-                for half in range(2):
-                    clear_pair(c, half, out)
+                clear_both(c, out)
                 if out == inner and c == LAYERS - 1:
                     finish_pair(1, 1)
         else:
-            for half in range(2):
-                clear_pair(c, half, inner)
+            clear_both(c, inner)
             if c == LAYERS - 1:
                 finish_pair(1, 1)
-            for half in range(2):
-                for way in range(2):
-                    take_halo(c, half, way)
-                clear_pair(c, half, outer)
+            clear_with_halo(c)
     finish_pair(0, LINES - 1)
 
     for i, o in enumerate(OFFSETS):
-        for c in range(2):
+        for c in range(CHUNKS):
             kv_copy(o, i, c).wait_send()
-        for c in range(CHUNKS):
             lat_copy(o, i, c).wait_send()
     for way in range(2):
 
@@ -522,16 +536,16 @@
             vmem((LAYERS, D, D), BF16),
             vmem((2, 9, LINES, SCAN), jnp.int32),
             vmem((SCAN * BLK * LINES + 72, CB), F32),
-            vmem((CHAN, 2, 2, BLK, 8, CB), BF16),
-            vmem((CHAN, 2, 2, BLK, 8, CB), BF16),
-            vmem((2, CB * 8, CB), F32),
-            vmem((2, CB * 8, CB), F32),
+            vmem((CHAN, CHUNKS, 2, BLK, STEP, CB), BF16),
+            vmem((CHAN, CHUNKS, 2, BLK, STEP, CB), BF16),
+            vmem((CHUNKS, CB * STEP, CB), F32),
+            vmem((CHUNKS, CB * STEP, CB), F32),
             vmem((HEADS * LAT, CB), BF16),
             vmem((LAT, CB), F32),
             vmem((STEP, LAT, D), BF16),
             vmem((CHAN, ROWS, LG, D), BF16),
-            vmem((LINES, PER, 2, LG, D), BF16),
-            vmem((2, DEEP, PER, 2, LG, D), BF16),
+            vmem((LINES, 2, PER, LG, D), BF16),
+            vmem((2, DEEP, 2, PER, LG, D), BF16),
             vmem((3, CB, CB), F32),
             vmem((CLEAR, 9, WIDE, CB), F32),
             vmem((LAYERS, CLEAR, FT, 9, WIDE, CB), F32),
@@ -543,7 +557,7 @@
             vmem((LINES, FT, LG * WIDE, CB), F32),
             vmem((LINES, SCAN, LG, D), BF16),
             dma((10,)),
-            dma((2, peers)), dma((2, peers)),
+            dma((CHUNKS, peers)), dma((CHUNKS, peers)),
             dma((CHUNKS, peers)), dma((CHUNKS, CHAN)),
             dma((CHUNKS, 2)), dma((CHUNKS, 2)),
             dma((2,)), dma((2,)),

time: 53.3 us -> 52.5 us (0.985)
  Pallas kernels: 50.6 us -> 50 us
    pallas_call x1, Pallas kernels: 50.6 us -> 50 us  [local(): pl.pallas_call(functools.partial(kernel, tracks), out_shape=jax.ShapeDtyp...]
where the time goes in v4:
time: 52.5 us; the launch traced here: 52.2 us
  Pallas kernels  50 us (95%)
  local copies, waits for them, and re-layouts  2.21 us (4%)
    pallas_call x1, Pallas kernels, local(): pl.pallas_call(functools.partial(kernel, tracks), out_shape=jax.ShapeDtyp...  50 us
    unnamed x1, local copies, waits for them, and re-layouts  2.21 us

profile of v4, /device:TPU:24, one launch (start us, length us, event | category | flops | bytes accessed | tf_op | source)
XLA Modules:
  0.0 52.2 jit_solution(13435639177633430155)
XLA Ops:
  0.0 50.0 %shard_map.100 = bf16[4,30,8,512]{3,2,1,0:T(8,128)(2,1)} custom-call(bf16[30,9,4,128]{3,2,1,0:T(4,128)(2,1)} %bitcast.3, bf16[9,128,128]{2,1,0:T(8,128)(2,1)} %wk_h.1, bf16[9,128,128]{2,1,0:T(8,128)(2,1)} %wv_h.1, bf16[64,512]{1,0:T(8,128)(2,1)} %q_h.1, s32[8,48]{1,0:T(8,128)} %bb_h.1, s32[8]{0:T(128)} %cnt_h.1, s32[9,4,30]{2,1,0:T(4,128)} %bitcast.5, ...), custom_call_target="tpu_custom_call" | custom-call | tf_op jit(solution)/shard_map/pallas_call | solution.py:521
  50.0 2.2 %copy.12 = bf16[4,30,8,512]{3,2,1,0:T(8,128)(2,1)} copy(bf16[4,30,8,512]{3,2,1,0:T(8,128)(2,1)} %shard_map.100) | data formatting | bytes 1966080

commit v5 on v4

--- a/solution.py
+++ b/solution.py
@@ -29,6 +29,7 @@
 EXCH = max(LAYERS - DEEP, 1)
 ALL = LINES + 2 * DEEP
 CLEAR = ALL - 2
+COLUMNS = 10
 MASKED = -1e30
 MESH = pl.DeviceIdType.MESH
 OFFSETS = ((2, 1), (2, 0), (1, 1), (3, 1), (1, 0), (3, 0), (0, 1))
@@ -414,14 +415,16 @@
                     halo_copy(c + 1, half, way).start()
 
     def finish_pair(first, apart):
-        def column(p, _):
-            for n in range(2):
-                for f in range(FT):
-                    rows = last[first + n * apart, f, pl.ds(p, LG, stride=WIDE), :]
-                    outb[first + n * apart, p, :, f * CB : (f + 1) * CB] = rows.astype(BF16)
+        def columns(group, _):
+            for d in range(COLUMNS):
+                p = group * COLUMNS + d
+                for n in range(2):
+                    for f in range(FT):
+                        rows = last[first + n * apart, f, pl.ds(p, LG, stride=WIDE), :]
+                        outb[first + n * apart, p, :, f * CB : (f + 1) * CB] = rows.astype(BF16)
             return 0
 
-        lax.fori_loop(0, SCAN, column, 0)
+        lax.fori_loop(0, SCAN // COLUMNS, columns, 0)
         for n in range(2):
             out_copy(first + n * apart).start()
 
@@ -479,19 +482,18 @@
 
     clear_both(0, inner)
     take_near()
-    for out in range(outer, -1, -1):
-        clear_both(0, out)
-    for c in range(1, LAYERS):
-        if c < DEEP:
-            for out in range(c, DEEP + 1):
-                clear_both(c, out)
-                if out == inner and c == LAYERS - 1:
-                    finish_pair(1, 1)
-        else:
-            clear_both(c, inner)
-            if c == LAYERS - 1:
-                finish_pair(1, 1)
-            clear_with_halo(c)
+
+    def up_to_halo(half, _):
+        for c in range(DEEP):
+            for out in range(outer, c - 1, -1):
+                clear_pair(c, half, out)
+        return 0
+
+    lax.fori_loop(0, 2, up_to_halo, 0)
+    clear_both(1, inner)
+    clear_both(2, inner)
+    finish_pair(1, 1)
+    clear_with_halo(2)
     finish_pair(0, LINES - 1)
 
     for i, o in enumerate(OFFSETS):

time: 52.5 us -> 51 us (0.971)
  Pallas kernels: 50 us -> 48.5 us
    pallas_call x1, Pallas kernels: 50 us -> 48.5 us  [local(): pl.pallas_call(functools.partial(kernel, tracks), out_shape=jax.ShapeDtyp...]
where the time goes in v5:
time: 51 us; the launch traced here: 50.7 us
  Pallas kernels  48.5 us (95%)
  local copies, waits for them, and re-layouts  2.21 us (4%)
    pallas_call x1, Pallas kernels, local(): pl.pallas_call(functools.partial(kernel, tracks), out_shape=jax.ShapeDtyp...  48.5 us
    unnamed x1, local copies, waits for them, and re-layouts  2.21 us

profile of v5, /device:TPU:24, one launch (start us, length us, event | category | flops | bytes accessed | tf_op | source)
XLA Modules:
  0.0 50.7 jit_solution(647129957153339414)
XLA Ops:
  0.0 48.5 %shard_map.100 = bf16[4,30,8,512]{3,2,1,0:T(8,128)(2,1)} custom-call(bf16[30,9,4,128]{3,2,1,0:T(4,128)(2,1)} %bitcast.3, bf16[9,128,128]{2,1,0:T(8,128)(2,1)} %wk_h.1, bf16[9,128,128]{2,1,0:T(8,128)(2,1)} %wv_h.1, bf16[64,512]{1,0:T(8,128)(2,1)} %q_h.1, s32[8,48]{1,0:T(8,128)} %bb_h.1, s32[8]{0:T(128)} %cnt_h.1, s32[9,4,30]{2,1,0:T(4,128)} %bitcast.5, ...), custom_call_target="tpu_custom_call" | custom-call | tf_op jit(solution)/shard_map/pallas_call | solution.py:523
  48.5 2.2 %copy.12 = bf16[4,30,8,512]{3,2,1,0:T(8,128)(2,1)} copy(bf16[4,30,8,512]{3,2,1,0:T(8,128)(2,1)} %shard_map.100) | data formatting | bytes 1966080

commit v6 on v5

--- a/solution.py
+++ b/solution.py
@@ -82,7 +82,7 @@
             )
         )
     ]
-    for load in loads:
+    for load in loads[:8]:
         load.start()
 
     xf[pl.ds(SCAN * BLK * LINES, 72), :] = jnp.zeros((72, CB), F32)
@@ -90,6 +90,8 @@
     xf[pl.ds(0, SCAN * BLK * LINES), :] = rad[...].astype(F32).reshape(SCAN * BLK * LINES, CB)
     loads[1].wait()
     loads[2].wait()
+    for load in loads[8:]:
+        load.start()
 
     for b in range(BLK):
         rows = jnp.concatenate(
@@ -122,7 +124,7 @@
         for i, o in enumerate(OFFSETS):
             kv_copy(o, i, c).start()
 
-    for load in loads[3:]:
+    for load in loads[3:8]:
         load.wait()
 
     def vm_copy(way):
@@ -321,6 +323,8 @@
             lat_copy(o, i, c).start()
         own_copy(c).start()
 
+    for load in loads[8:]:
+        load.wait()
     for c in range(CHUNKS):
         for i in reversed(range(len(OFFSETS))):
             o = OFFSETS[i]

time: 51 us -> 50.8 us (level)
  no operation moved by 1% of the time
where the time goes in v6:
time: 50.8 us; the launch traced here: 50.6 us
  Pallas kernels  48.4 us (95%)
  local copies, waits for them, and re-layouts  2.21 us (4%)
    pallas_call x1, Pallas kernels, local(): pl.pallas_call(functools.partial(kernel, tracks), out_shape=jax.ShapeDtyp...  48.4 us
    unnamed x1, local copies, waits for them, and re-layouts  2.21 us

profile of v6, /device:TPU:24, one launch (start us, length us, event | category | flops | bytes accessed | tf_op | source)
XLA Modules:
  0.0 50.6 jit_solution(11056550946943653198)
XLA Ops:
  0.0 48.4 %shard_map.100 = bf16[4,30,8,512]{3,2,1,0:T(8,128)(2,1)} custom-call(bf16[30,9,4,128]{3,2,1,0:T(4,128)(2,1)} %bitcast.3, bf16[9,128,128]{2,1,0:T(8,128)(2,1)} %wk_h.1, bf16[9,128,128]{2,1,0:T(8,128)(2,1)} %wv_h.1, bf16[64,512]{1,0:T(8,128)(2,1)} %q_h.1, s32[8,48]{1,0:T(8,128)} %bb_h.1, s32[8]{0:T(128)} %cnt_h.1, s32[9,4,30]{2,1,0:T(4,128)} %bitcast.5, ...), custom_call_target="tpu_custom_call" | custom-call | tf_op jit(solution)/shard_map/pallas_call | solution.py:527
  48.4 2.2 %copy.12 = bf16[4,30,8,512]{3,2,1,0:T(8,128)(2,1)} copy(bf16[4,30,8,512]{3,2,1,0:T(8,128)(2,1)} %shard_map.100) | data formatting | bytes 1966080
